TPU v7x, 32 devices: a whole 2x2x4 slice. The times are simulated.
32 devices in a mesh: grp: 4 (over z), blk: 8 (over y, x, core).
Axes of the slice: x: 2, y: 2, z: 4, core: 2. Of those that a mesh axis runs over, the one named last changes fastest.
Arguments:
- modes: bfloat16 [3, 256, 8, 32, 128], P(None, None, 'grp', 'blk'), may hold values from -6 to 6
- metric: float32 [3, 8, 32, 128], P(None, 'grp', 'blk'), may hold values from 0.5 to 2
- block_map: int32 [8, 32, 128], P('grp', 'blk'), may hold values from 0 to 15
- flags: int32 [8, 32, 128], P('grp', 'blk'), may hold values from 0 to 2
- region_scale: float32 [16], replicated, may hold values from 0.5 to 2
Outputs:
- tensor: float32 [8, 256, 256], P(None, 'grp', 'blk')
All inputs are finite; a program needn't handle non-finite values.
Results may differ from a plain program's by a relative error of at most 0.0042.
Values may be sent and summed in bfloat16 or wider, within the bound.
No kernel may reach another device: no remote copies, remote signals or barrier semaphores. Data moves between devices by JAX's collectives and lax.ppermute only.
A program may use at most 64 MiB of HBM per device.

v0:
```python
import jax
import jax.numpy as jnp
from jax import lax
from jax.sharding import PartitionSpec as P

KS = 8


def with_halo(cells, sides, width):
    for axis, dim in sides:
        count = lax.axis_size(axis)
        ends = count - 1
        head = lax.slice_in_dim(cells, 0, width, axis=dim)
        tail = lax.slice_in_dim(cells, cells.shape[dim] - width, cells.shape[dim], axis=dim)
        cells = jnp.concatenate(
            [
                lax.ppermute(tail, axis, [(i, (i + 1) % count) for i in range(ends)]),
                cells,
                lax.ppermute(head, axis, [((i + 1) % count, i) for i in range(ends)]),
            ],
            axis=dim,
        )
    return cells


def stencil(padded, metric):
    gx = 0.5 * (padded[:, :, 2:, 1:-1, 1:-1] - padded[:, :, :-2, 1:-1, 1:-1]) * metric[0]
    gy = 0.5 * (padded[:, :, 1:-1, 2:, 1:-1] - padded[:, :, 1:-1, :-2, 1:-1]) * metric[1]
    gz = 0.5 * (padded[:, :, 1:-1, 1:-1, 2:] - padded[:, :, 1:-1, 1:-1, :-2]) * metric[2]
    return jnp.stack([gx, gy, gz])


def weights(block_map, flags, region_scale, metric, norm):
    labels = jnp.arange(region_scale.shape[0], dtype=jnp.int32)[:, None, None, None]
    scale = jnp.sum(
        jnp.where(block_map[None] == labels, region_scale[:, None, None, None], jnp.float32(0.0)),
        axis=0,
    )
    fluid = jnp.where(
        flags == 0, jnp.float32(1.0), jnp.where(flags == 1, jnp.float32(0.0), jnp.float32(0.5))
    )
    return scale * fluid * norm / (metric[0] * metric[1] * metric[2])


def local(modes, metric, block_map, flags, region_scale):
    groups = lax.axis_size("grp")
    blocks = lax.axis_size("blk")
    count = modes.shape[1]
    total_cells = modes.shape[2] * groups * modes.shape[3] * blocks * modes.shape[4]
    norm = float(total_cells) ** (-0.5)
    slab = modes[:, :KS]
    rimmed = with_halo(slab, (("grp", 2), ("blk", 3)), 1)
    padded = jnp.pad(rimmed.astype(jnp.float32), ((0, 0), (0, 0), (0, 0), (0, 0), (1, 1)))
    grads = stencil(padded, metric)
    weight = weights(block_map, flags, region_scale, metric, norm).reshape(-1)
    flat = modes.reshape(3, count, -1)
    flat_wide = flat.astype(jnp.float32)
    grads = grads.reshape(3, 3, KS, -1)
    partials = []
    for k in range(KS):
        grad_k = grads[:, :, k]
        mixed = flat_wide[0][None] * grad_k[:, 0][:, None]
        mixed = mixed + flat_wide[1][None] * grad_k[:, 1][:, None]
        mixed = mixed + flat_wide[2][None] * grad_k[:, 2][:, None]
        tested = (weight[None, None] * mixed).astype(jnp.bfloat16)
        partials.append(
            lax.dot_general(
                tested, flat, (((0, 2), (0, 2)), ((), ())), preferred_element_type=jnp.float32
            )
        )
    partial_value = jnp.stack(partials)
    inner = lax.psum_scatter(partial_value, "blk", scatter_dimension=2, tiled=True)
    result = lax.psum_scatter(inner, "grp", scatter_dimension=1, tiled=True)
    return result


def solution(mesh):
    return jax.shard_map(
        local,
        mesh=mesh,
        in_specs=(
            P(None, None, "grp", "blk", None),
            P(None, "grp", "blk", None),
            P("grp", "blk", None),
            P("grp", "blk", None),
            P(),
        ),
        out_specs=P(None, "grp", "blk"),
        check_vma=False,
    )
```

profile of v0, /device:TPU:0, one launch (start us, length us, event | category | flops | bytes accessed | tf_op | source)
XLA Modules:
  0.0 131.9 jit_solution(16324299882136081485)
XLA Ops:
  6.5 0.0 copy-start.2
  6.5 0.0 reduce-scatter.5.cloned.1.call-start
  6.5 0.8 fusion.84
  7.3 5.0 %collective-permute-start = (bf16[3,8,1,4,128]{4,3,2,1,0:T(4,128)(2,1)S(1)}, bf16[3,8,1,4,128]{4,3,2,1,0:T(4,128)(2,1)S(1)}, u32[]{:S(2)}, u32[]{:S(2)}) collective-permute-start(bf16[3,8,1,4,128]{4,3,2,1,0:T(4,128)(2,1)S(1)} %get-tuple-element.8), channel_id=1, source_target_pairs={{0,8},{8,16},{16,24},{1,9},{9,17},{17,25},{2,10},{10,18},{18,26},{... | collective-permute-start | bytes 73736 | tf_op jit(solution)/shard_map/ppermute | solution.py:17
  12.3 1.3 collective-permute-start.1
  13.6 2.8 %reshape.24 = bf16[3,256,1024]{2,1,0:T(8,128)(2,1)S(1)} reshape(bf16[3,256,2,4,128]{4,3,2,1,0:T(4,128)(2,1)} %param.5) | data formatting | bytes 3145728 | tf_op jit(solution)/shard_map/reshape | solution.py:56
  16.4 0.0 copy-done.2
  16.4 0.4 convert_element_type.32
  16.8 0.0 copy-start.3
  16.8 0.0 copy-start.5
  16.9 0.0 copy-start.4
  16.9 1.5 %slice_bitcast_fusion.2 = (f32[256,1024]{1,0:T(8,128)S(1)}, f32[256,1024]{1,0:T(8,128)}, f32[256,1024]{1,0:T(8,128)}) fusion(f32[3,256,1024]{2,1,0:T(8,128)S(1)} %convert_element_type.32), kind=kLoop, calls=%fused_computation.90 | loop fusion | bytes 6291456 | tf_op jit(solution)/shard_map/mul | solution.py:62
  18.4 0.0 copy-done.3
  18.4 0.0 copy-done.5
  18.4 0.1 select_reduce_fusion
  18.5 0.8 slice.182
  19.3 0.0 collective-permute-done
  19.3 0.0 collective-permute-done.1
  19.3 0.1 pad_maximum_fusion
  19.4 0.1 fusion.86
  19.5 1.5 %collective-permute-start.2 = (bf16[3,8,4,1,128]{4,3,2,1,0:T(2,128)(2,1)S(1)}, bf16[3,8,4,1,128]{4,3,2,1,0:T(2,128)(2,1)S(1)}, u32[]{:S(2)}, u32[]{:S(2)}) collective-permute-start(bf16[3,8,4,1,128]{4,3,2,1,0:T(2,128)(2,1)S(1)} %get-tuple-element.21), channel_id=1, source_target_pairs={{0,1},{1,2},{2,3},{3,4},{4,5},{5,6},{6,7},{8,9},{9,10},{10,11},{11... | collective-permute-start | bytes 73736 | tf_op jit(solution)/shard_map/ppermute | solution.py:17
  21.0 1.3 collective-permute-start.3
  22.3 0.0 copy-done.4
  22.3 0.0 collective-permute-done.2
  22.3 3.3 %collective-permute-done.3 = bf16[3,8,4,1,128]{4,3,2,1,0:T(2,128)(2,1)S(1)} collective-permute-done((bf16[3,8,4,1,128]{4,3,2,1,0:T(2,128)(2,1)S(1)}, bf16[3,8,4,1,128]{4,3,2,1,0:T(2,128)(2,1)S(1)}, u32[]{:S(2)}, u32[]{:S(2)}) %collective-permute-start.3) | collective-permute-done | bytes 24608 | tf_op jit(solution)/shard_map/ppermute | solution.py:19
  25.7 0.2 maximum_convert_fusion
  25.8 0.2 fusion.81
  26.2 0.2 fusion.85
  27.2 0.0 copy-start
  27.2 0.0 copy-start.1
  27.2 3.4 %fusion.79 = f32[8,256,256]{2,1,0:T(8,128)} fusion(bf16[3,256,1024]{2,1,0:T(8,128)(2,1)S(1)} %reshape.24, f32[3,1024]{1,0:T(4,128)S(1)} %bitcast.156, f32[256,1024]{1,0:T(8,128)} %get-tuple-element.6, f32[3,1024]{1,0:T(4,128)S(1)} %bitcast.157, f32[256,1024]{1,0:T(8,128)} %get-tuple-element.7, f32[3,1024]{1,0:T(4,128)S(1)} %bitcast.158, ...), kind=kOutput, calls=%fused_computation.87 | convolution fusion | flops 408158208 | bytes 5021696 | tf_op jit(solution)/shard_map/dot_general | solution.py:67
  30.5 0.0 copy-done
  30.5 0.0 copy-done.1
  30.5 1.8 %fusion.77 = f32[8,256,256]{2,1,0:T(8,128)} fusion(f32[8,256,256]{2,1,0:T(8,128)} %fusion.79, bf16[3,256,1024]{2,1,0:T(8,128)(2,1)S(1)} %reshape.24, f32[3,1024]{1,0:T(4,128)S(1)} %bitcast.159, f32[3,1024]{1,0:T(4,128)S(1)} %bitcast.160, f32[3,1024]{1,0:T(4,128)S(1)} %bitcast.161, f32[256,1024]{1,0:T(8,128)S(1)} %copy-done, f32[256,1024]{1,0:T(8,128)S(1)} %copy-done.1, ...), kind=kOutput, calls=%fused_computation.85 | convolution fusion | flops 408158208 | bytes 5021696 | tf_op jit(solution)/shard_map/dot_general | solution.py:67
  32.4 1.8 %fusion.75 = f32[8,256,256]{2,1,0:T(8,128)} fusion(f32[8,256,256]{2,1,0:T(8,128)} %fusion.77, bf16[3,256,1024]{2,1,0:T(8,128)(2,1)S(1)} %reshape.24, f32[3,1024]{1,0:T(4,128)S(1)} %bitcast.162, f32[3,1024]{1,0:T(4,128)S(1)} %bitcast.163, f32[3,1024]{1,0:T(4,128)S(1)} %bitcast.164, f32[256,1024]{1,0:T(8,128)S(1)} %copy-done, f32[256,1024]{1,0:T(8,128)S(1)} %copy-done.1, ...), kind=kOutput, calls=%fused_computation.83 | convolution fusion | flops 408158208 | bytes 5021696 | tf_op jit(solution)/shard_map/dot_general | solution.py:67
  34.2 1.8 %fusion.73 = f32[8,256,256]{2,1,0:T(8,128)} fusion(f32[8,256,256]{2,1,0:T(8,128)} %fusion.75, bf16[3,256,1024]{2,1,0:T(8,128)(2,1)S(1)} %reshape.24, f32[3,1024]{1,0:T(4,128)S(1)} %bitcast.165, f32[3,1024]{1,0:T(4,128)S(1)} %bitcast.166, f32[3,1024]{1,0:T(4,128)S(1)} %bitcast.167, f32[256,1024]{1,0:T(8,128)S(1)} %copy-done, f32[256,1024]{1,0:T(8,128)S(1)} %copy-done.1, ...), kind=kOutput, calls=%fused_computation.81 | convolution fusion | flops 408158208 | bytes 5021696 | tf_op jit(solution)/shard_map/dot_general | solution.py:67
  36.0 1.8 %fusion.71 = f32[8,256,256]{2,1,0:T(8,128)} fusion(f32[8,256,256]{2,1,0:T(8,128)} %fusion.73, bf16[3,256,1024]{2,1,0:T(8,128)(2,1)S(1)} %reshape.24, f32[3,1024]{1,0:T(4,128)S(1)} %bitcast.168, f32[3,1024]{1,0:T(4,128)S(1)} %bitcast.169, f32[3,1024]{1,0:T(4,128)S(1)} %bitcast.170, f32[256,1024]{1,0:T(8,128)S(1)} %copy-done, f32[256,1024]{1,0:T(8,128)S(1)} %copy-done.1, ...), kind=kOutput, calls=%fused_computation.79 | convolution fusion | flops 408158208 | bytes 5021696 | tf_op jit(solution)/shard_map/dot_general | solution.py:67
  37.8 1.8 %fusion.69 = f32[8,256,256]{2,1,0:T(8,128)} fusion(f32[8,256,256]{2,1,0:T(8,128)} %fusion.71, bf16[3,256,1024]{2,1,0:T(8,128)(2,1)S(1)} %reshape.24, f32[3,1024]{1,0:T(4,128)S(1)} %bitcast.171, f32[3,1024]{1,0:T(4,128)S(1)} %bitcast.172, f32[3,1024]{1,0:T(4,128)S(1)} %bitcast.173, f32[256,1024]{1,0:T(8,128)S(1)} %copy-done, f32[256,1024]{1,0:T(8,128)S(1)} %copy-done.1, ...), kind=kOutput, calls=%fused_computation.77 | convolution fusion | flops 408158208 | bytes 5021696 | tf_op jit(solution)/shard_map/dot_general | solution.py:67
  39.6 1.8 %fusion.67 = f32[8,256,256]{2,1,0:T(8,128)} fusion(f32[8,256,256]{2,1,0:T(8,128)} %fusion.69, bf16[3,256,1024]{2,1,0:T(8,128)(2,1)S(1)} %reshape.24, f32[3,1024]{1,0:T(4,128)S(1)} %bitcast.174, f32[3,1024]{1,0:T(4,128)S(1)} %bitcast.175, f32[3,1024]{1,0:T(4,128)S(1)} %bitcast.176, f32[256,1024]{1,0:T(8,128)S(1)} %copy-done, f32[256,1024]{1,0:T(8,128)S(1)} %copy-done.1, ...), kind=kOutput, calls=%fused_computation.75 | convolution fusion | flops 408158208 | bytes 5021696 | tf_op jit(solution)/shard_map/dot_general | solution.py:67
  41.5 1.8 %fusion.65 = f32[8,256,256]{2,1,0:T(8,128)} fusion(f32[8,256,256]{2,1,0:T(8,128)} %fusion.67, bf16[3,256,1024]{2,1,0:T(8,128)(2,1)S(1)} %reshape.24, f32[3,1024]{1,0:T(4,128)S(1)} %bitcast.177, f32[3,1024]{1,0:T(4,128)S(1)} %bitcast.178, f32[3,1024]{1,0:T(4,128)S(1)} %bitcast.179, f32[256,1024]{1,0:T(8,128)S(1)} %copy-done, f32[256,1024]{1,0:T(8,128)S(1)} %copy-done.1, ...), kind=kOutput, calls=%fused_computation.73 | convolution fusion | flops 408158208 | bytes 5021696 | tf_op jit(solution)/shard_map/dot_general | solution.py:67
  43.3 3.0 %copy.11 = f32[8,256,256]{1,0,2:T(8,128)} copy(f32[8,256,256]{2,1,0:T(8,128)} %fusion.65) | data formatting | bytes 4194304 | tf_op jit(solution)/shard_map/stack | solution.py:71
  46.3 0.0 reduce-scatter.5.cloned.1.call-update
  46.3 0.2 reduce-scatter.7.cloned.1.call-start
  46.6 45.7 %reduce-scatter.5.cloned.1.call-done = f32[8,256,32]{1,0,2:T(8,128)} async-done(((f32[8,256,256]{1,0,2:T(8,128)}), f32[8,256,32]{1,0,2:T(8,128)}) %reduce-scatter.5.cloned.1.call-update) | async-done | bytes 262160 | tf_op jit(solution)/shard_map/reduce_scatter | solution.py:72
  92.3 5.2 %copy.13 = f32[8,256,32]{0,2,1:T(8,128)} copy(f32[8,256,32]{1,0,2:T(8,128)} %reduce-scatter.5.cloned.1.call-done) | data formatting | bytes 524288
  97.5 4.7 %reshape.33 = f32[256,256]{1,0:T(8,128)} reshape(f32[256,32,8]{2,1,0:T(8,128)} %bitcast.154) | data formatting | bytes 524288
  102.2 0.0 reduce-scatter.7.cloned.1.call-update
  102.2 20.2 %reduce-scatter.7.cloned.1.call-done = f32[64,256]{1,0:T(8,128)} async-done(((f32[256,256]{1,0:T(8,128)}), f32[64,256]{1,0:T(8,128)}) %reduce-scatter.7.cloned.1.call-update) | async-done | bytes 65552
  122.3 1.4 %reshape.34 = f32[64,32,8]{2,1,0:T(8,128)S(1)} reshape(f32[64,256]{1,0:T(8,128)} %reduce-scatter.7.cloned.1.call-done) | data formatting | bytes 131072
  123.8 1.3 copy.12
  (44 shorter events, 0.6 us)
Async XLA Ops:
  6.5 9.9 %copy-start.2 = (f32[3,2,4,128]{3,2,1,0:T(4,128)S(1)}, f32[3,2,4,128]{3,2,1,0:T(4,128)}, u32[]{:S(2)}) copy-start(f32[3,2,4,128]{3,2,1,0:T(4,128)} %param.6) | copy-start | bytes 36868
  6.5 85.7 %reduce-scatter.5.cloned.1.call-start = ((), (), s32[]{:S(2)}) async-start(), calls=%async_computation.2 | async-start | bytes 2359296 | tf_op jit(solution)/shard_map/reduce_scatter | solution.py:72
  7.3 12.0 %collective-permute-start = (bf16[3,8,1,4,128]{4,3,2,1,0:T(4,128)(2,1)S(1)}, bf16[3,8,1,4,128]{4,3,2,1,0:T(4,128)(2,1)S(1)}, u32[]{:S(2)}, u32[]{:S(2)}) collective-permute-start(bf16[3,8,1,4,128]{4,3,2,1,0:T(4,128)(2,1)S(1)} %get-tuple-element.8), channel_id=1, source_target_pairs={{0,8},{8,16},{16,24},{1,9},{9,17},{17,25},{2,10},{10,18},{18,26},{... | collective-permute-start | bytes 73736 | tf_op jit(solution)/shard_map/ppermute | solution.py:17
  12.3 7.0 %collective-permute-start.1 = (bf16[3,8,1,4,128]{4,3,2,1,0:T(4,128)(2,1)S(1)}, bf16[3,8,1,4,128]{4,3,2,1,0:T(4,128)(2,1)S(1)}, u32[]{:S(2)}, u32[]{:S(2)}) collective-permute-start(bf16[3,8,1,4,128]{4,3,2,1,0:T(4,128)(2,1)S(1)} %get-tuple-element.9), channel_id=1, source_target_pairs={{8,0},{16,8},{24,16},{9,1},{17,9},{25,17},{10,2},{18,10},{26,18},{... | collective-permute-start | bytes 73736 | tf_op jit(solution)/shard_map/ppermute | solution.py:19
  16.8 1.6 %copy-start.3 = (s32[2,4,128]{2,1,0:T(4,128)S(1)}, s32[2,4,128]{2,1,0:T(4,128)}, u32[]{:S(2)}) copy-start(s32[2,4,128]{2,1,0:T(4,128)} %param.7) | copy-start | bytes 12292
  16.8 1.6 %copy-start.5 = (f32[16]{0:T(128)S(1)}, f32[16]{0:T(128)}, u32[]{:S(2)}) copy-start(f32[16]{0:T(128)} %param.9) | copy-start | bytes 196
  16.9 5.4 %copy-start.4 = (s32[2,4,128]{2,1,0:T(4,128)S(1)}, s32[2,4,128]{2,1,0:T(4,128)}, u32[]{:S(2)}) copy-start(s32[2,4,128]{2,1,0:T(4,128)} %param.8) | copy-start | bytes 12292
  19.5 2.8 %collective-permute-start.2 = (bf16[3,8,4,1,128]{4,3,2,1,0:T(2,128)(2,1)S(1)}, bf16[3,8,4,1,128]{4,3,2,1,0:T(2,128)(2,1)S(1)}, u32[]{:S(2)}, u32[]{:S(2)}) collective-permute-start(bf16[3,8,4,1,128]{4,3,2,1,0:T(2,128)(2,1)S(1)} %get-tuple-element.21), channel_id=1, source_target_pairs={{0,1},{1,2},{2,3},{3,4},{4,5},{5,6},{6,7},{8,9},{9,10},{10,11},{11... | collective-permute-start | bytes 73736 | tf_op jit(solution)/shard_map/ppermute | solution.py:17
  21.0 4.7 %collective-permute-start.3 = (bf16[3,8,4,1,128]{4,3,2,1,0:T(2,128)(2,1)S(1)}, bf16[3,8,4,1,128]{4,3,2,1,0:T(2,128)(2,1)S(1)}, u32[]{:S(2)}, u32[]{:S(2)}) collective-permute-start(bf16[3,8,4,1,128]{4,3,2,1,0:T(2,128)(2,1)S(1)} %get-tuple-element.22), channel_id=1, source_target_pairs={{1,0},{2,1},{3,2},{4,3},{5,4},{6,5},{7,6},{9,8},{10,9},{11,10},{12... | collective-permute-start | bytes 73736 | tf_op jit(solution)/shard_map/ppermute | solution.py:19
  27.2 3.4 %copy-start = (f32[256,1024]{1,0:T(8,128)S(1)}, f32[256,1024]{1,0:T(8,128)}, u32[]{:S(2)}) copy-start(f32[256,1024]{1,0:T(8,128)} %get-tuple-element.6) | copy-start | bytes 3145732
  27.2 3.4 %copy-start.1 = (f32[256,1024]{1,0:T(8,128)S(1)}, f32[256,1024]{1,0:T(8,128)}, u32[]{:S(2)}) copy-start(f32[256,1024]{1,0:T(8,128)} %get-tuple-element.7) | copy-start | bytes 3145732
  46.3 76.0 %reduce-scatter.7.cloned.1.call-start = ((), (), s32[]{:S(2)}) async-start(), calls=%async_computation.3 | async-start | bytes 327680
Sparse Core Ops, SparseCore 0:
  46.5 45.7 reduce-scatter.4
  102.3 19.9 reduce-scatter.6
where the time goes:
time: 132 us
  waiting for transfers between devices  69.3 us (52%)
  local copies, waits for them, and re-layouts  22.5 us (17%)
  matrix products  16.1 us (12%)
  between operations  13.9 us (11%)
  starting transfers between devices  9.23 us (7%)
    reduce_scatter x1, waiting for transfers between devices, local(): lax.psum_scatter(partial_value, 'blk', scatter_dimension=2, tiled=True)  45.7 us
    unnamed x3, waiting for transfers between devices  20.2 us
    dot_general x8, matrix products, local(): lax.dot_general(tested, flat, (((0, 2), (0, 2)), ((), ())), preferred_ele...  16.1 us
    unnamed x45, local copies, waits for them, and re-layouts  11.6 us
    ppermute x2, starting transfers between devices, with_halo(): lax.ppermute(tail, axis, [(i, (i + 1) % count) for i in range(ends)])  6.42 us
    ppermute x2, waiting for transfers between devices, with_halo(): lax.ppermute(head, axis, [((i + 1) % count, i) for i in range(ends)])  3.35 us
    another operation x1, local copies, waits for them, and re-layouts, local(): partial_value = jnp.stack(partials)  3.03 us
    reshape x1, local copies, waits for them, and re-layouts, local(): flat = modes.reshape(3, count, -1)  2.83 us
  transfers between devices with their start and end apart: 6, of which 3 were waited for; matrix products, arithmetic and copies ran while one was open for 4% of the time, Pallas kernels for 0%

commit v1 on v0

v1 whole, which is shorter than its diff:
```python
import jax
import jax.numpy as jnp
import numpy as np
from jax import lax
from jax.experimental import pallas as pl
from jax.experimental.pallas import tpu as pltpu
from jax.sharding import PartitionSpec as P

KS = 8
LANES = 128
TILE = 64
F32 = jnp.float32
BF16 = jnp.bfloat16


def halving_masks(blocks):
    bits = [1 << b for b in range(1, blocks.bit_length() - 1)]
    turn = len(bits) // 2
    return [bits, bits[turn:] + bits[:turn]]


def block_order(blocks, me):
    masks = halving_masks(blocks)
    depth = blocks.bit_length() - 1
    table = np.zeros((2, blocks), np.int32)
    for odd in range(2):
        for p in range(blocks):
            top = p >> (depth - 1)
            pattern = top
            for t, mask in enumerate(masks[odd ^ top]):
                if (p >> (depth - 2 - t)) & 1:
                    pattern ^= mask
            table[odd, p] = pattern
    return me ^ jnp.where(me % 2 == 1, jnp.asarray(table[1]), jnp.asarray(table[0]))


def x_halo(slab):
    count = lax.axis_size("grp")
    up = [(i, i + 1) for i in range(count - 1)]
    down = [(i + 1, i) for i in range(count - 1)]
    return (
        lax.ppermute(slab[:, :, -1:], "grp", up),
        lax.ppermute(slab[:, :, :1], "grp", down),
    )


def y_halo(slab, odd):
    count = lax.axis_size("blk")
    first, last = slab[:, :, :, :1], slab[:, :, :, -1:]
    far = [(i, i + 1) for i in range(1, count - 1, 2)]
    near = [(i, i + 1) for i in range(0, count - 1, 2)]
    far_in = lax.ppermute(jnp.where(odd, last, first), "blk", far + [(b, a) for a, b in far])
    near_in = lax.ppermute(jnp.where(odd, first, last), "blk", near + [(b, a) for a, b in near])
    return jnp.where(odd, near_in, far_in), jnp.where(odd, far_in, near_in)


def weights(block_map, flags, region_scale, metric, norm):
    labels = jnp.arange(region_scale.shape[0], dtype=jnp.int32)[:, None, None, None]
    scale = jnp.sum(
        jnp.where(block_map[None] == labels, region_scale[:, None, None, None], jnp.float32(0.0)),
        axis=0,
    )
    fluid = jnp.where(
        flags == 0, jnp.float32(1.0), jnp.where(flags == 1, jnp.float32(0.0), jnp.float32(0.5))
    )
    return scale * fluid * norm / (metric[0] * metric[1] * metric[2])


def relay_kernel(order_ref, rows_ref, wide_ref, adv_ref, flat_ref):
    _, cells, count, _ = wide_ref.shape
    blocks = order_ref.shape[0]
    width = count // blocks
    flat_ref[...] = rows_ref[0].astype(F32)
    for r in range(cells):
        wide_ref[0, r] = flat_ref[pl.ds(r, count, stride=cells), :]
    for p in range(blocks):
        start = pl.multiple_of(order_ref[p] * width, width)
        for r in range(cells):
            part = wide_ref[0, r, pl.ds(start, width), :]
            adv_ref[p * width : (p + 1) * width, r * LANES : (r + 1) * LANES] = part.astype(BF16)


def relay(order, rows, count, cells):
    comps = rows.shape[0]
    return pl.pallas_call(
        relay_kernel,
        grid_spec=pltpu.PrefetchScalarGridSpec(
            num_scalar_prefetch=1,
            grid=(comps,),
            in_specs=[pl.BlockSpec((1, count * cells, LANES), lambda c, _: (c, 0, 0))],
            out_specs=[
                pl.BlockSpec((1, cells, count, LANES), lambda c, _: (c, 0, 0, 0)),
                pl.BlockSpec((count, cells * LANES), lambda c, _: (0, c)),
            ],
            scratch_shapes=[pltpu.VMEM((count * cells, LANES), F32)],
        ),
        out_shape=[
            jax.ShapeDtypeStruct((comps, cells, count, LANES), F32),
            jax.ShapeDtypeStruct((count, comps * cells * LANES), BF16),
        ],
        name="relay",
    )(order, rows)


def tensor_kernel(wide_ref, adv_ref, diff_ref, scale_ref, keep_ref, send_ref, grad_ref, t0_ref, t1_ref):
    comps, cells, count, _ = wide_ref.shape
    dims = diff_ref.shape[0]
    half = keep_ref.shape[1]
    for d in range(dims):
        for c in range(comps):
            for k in range(KS):
                grad_ref[(k * dims + d) * comps + c] = diff_ref[d, c * KS + k] * scale_ref[d]

    def build(k, t_ref):
        for r in range(cells):
            for i in range(0, count, TILE):
                a = [wide_ref[c, r, i : i + TILE, :] for c in range(comps)]
                for d in range(dims):
                    at = (k * dims + d) * comps
                    g = [grad_ref[at + c, pl.ds(r, 1), :] for c in range(comps)]
                    total = a[0] * g[0]
                    for c in range(1, comps):
                        total = total + a[c] * g[c]
                    col = (d * cells + r) * LANES
                    t_ref[i : i + TILE, col : col + LANES] = total.astype(BF16)

    def contract(k, t_ref):
        out = lax.dot_general(
            adv_ref[...], t_ref[...], (((1,), (1,)), ((), ())), preferred_element_type=F32
        )
        keep_ref[k] = out[:half]
        send_ref[k] = out[half:].astype(BF16)

    build(0, t0_ref)

    def step(n, carry):
        build(2 * n + 1, t1_ref)
        contract(2 * n, t0_ref)
        build(2 * n + 2, t0_ref)
        contract(2 * n + 1, t1_ref)
        return carry

    lax.fori_loop(0, KS // 2 - 1, step, 0)
    build(KS - 1, t1_ref)
    contract(KS - 2, t0_ref)
    contract(KS - 1, t1_ref)


def tensor_parts(wide, adv, diff, scale):
    comps, cells, count, _ = wide.shape
    half = count // 2
    depth = adv.shape[1]
    return pl.pallas_call(
        tensor_kernel,
        out_shape=[
            jax.ShapeDtypeStruct((KS, half, count), F32),
            jax.ShapeDtypeStruct((KS, half, count), BF16),
        ],
        scratch_shapes=[
            pltpu.VMEM((KS * comps * comps, cells, LANES), F32),
            pltpu.VMEM((count, depth), BF16),
            pltpu.VMEM((count, depth), BF16),
        ],
        name="tensor_parts",
    )(wide, adv, diff, scale)


def pack_kernel(me_ref, keep_ref, recv_ref, own_ref, *rest):
    sends, chunk_ref = rest[:-1], rest[-1]
    groups = len(sends) + 1
    width = keep_ref.shape[2] // groups
    fold = KS // own_ref.shape[0]
    me = me_ref[0]
    for row in range(own_ref.shape[0]):
        full = [
            keep_ref[row * fold + q] + recv_ref[row * fold + q].astype(F32) for q in range(fold)
        ]
        for z in range(groups):
            parts = [f[:, z * width : (z + 1) * width] for f in full]
            chunk_ref[me ^ z, row] = parts[0] if fold == 1 else jnp.concatenate(parts, axis=1)
    own_ref[...] = chunk_ref[0]
    for t, send in enumerate(sends):
        send[...] = chunk_ref[t + 1].astype(BF16)


def pack(me, keep, recv, groups):
    _, rows, count = keep.shape
    fold = max(1, LANES // (count // groups))
    shape = (KS // fold, rows, fold * count // groups)
    return pl.pallas_call(
        pack_kernel,
        in_specs=[
            pl.BlockSpec(memory_space=pltpu.SMEM),
            pl.BlockSpec(memory_space=pltpu.VMEM),
            pl.BlockSpec(memory_space=pltpu.VMEM),
        ],
        out_shape=[jax.ShapeDtypeStruct(shape, F32)]
        + [jax.ShapeDtypeStruct(shape, BF16)] * (groups - 1),
        scratch_shapes=[pltpu.VMEM((groups,) + shape, F32)],
        name="pack",
    )(me, keep, recv)


def finish_kernel(own_ref, *rest):
    recvs, out_ref = rest[:-1], rest[-1]
    fold = KS // own_ref.shape[0]
    width = out_ref.shape[1]
    for row in range(own_ref.shape[0]):
        total = own_ref[row]
        for recv in recvs:
            total = total + recv[row].astype(F32)
        turned = total.T
        for q in range(fold):
            out_ref[row * fold + q] = turned[q * width : (q + 1) * width, :]


def finish(own, recvs, width):
    rows = own.shape[1]
    return pl.pallas_call(
        finish_kernel,
        out_shape=jax.ShapeDtypeStruct((KS, width, rows), F32),
        name="finish",
    )(own, *recvs)


def local(modes, metric, block_map, flags, region_scale):
    groups = lax.axis_size("grp")
    blocks = lax.axis_size("blk")
    comps, count, nx, ny, nz = modes.shape
    cells = nx * ny
    total_cells = nx * groups * ny * blocks * nz
    norm = float(total_cells) ** (-0.5)
    me = lax.axis_index("blk")
    odd = me % 2 == 1

    slab = modes[:, :KS]
    x_prev, x_next = x_halo(slab)
    y_prev, y_next = y_halo(slab, odd)
    rows = modes.reshape(comps, count * cells, nz)
    wide, adv = relay(block_order(blocks, me), rows, count, cells)

    weight = weights(block_map, flags, region_scale, metric, norm)
    scale = (0.5 * metric * weight).reshape(comps, cells, nz)
    zero = jnp.zeros_like(slab[..., :1])

    def between(after, before):
        return after.astype(F32) - before.astype(F32)

    diff = jnp.stack(
        [
            between(
                jnp.concatenate([slab[:, :, 1:], x_next], 2),
                jnp.concatenate([x_prev, slab[:, :, :-1]], 2),
            ),
            between(
                jnp.concatenate([slab[:, :, :, 1:], y_next], 3),
                jnp.concatenate([y_prev, slab[:, :, :, :-1]], 3),
            ),
            between(
                jnp.concatenate([slab[..., 1:], zero], 4),
                jnp.concatenate([zero, slab[..., :-1]], 4),
            ),
        ]
    ).reshape(3, comps * KS, cells, nz)

    keep, send = tensor_parts(wide, adv, diff, scale)
    masks = halving_masks(blocks)
    steps = [[1, 1]] + [list(pair) for pair in zip(*masks)]
    for n, pair in enumerate(steps):
        recv = lax.ppermute(send, "blk", [(i, i ^ pair[i % 2]) for i in range(blocks)])
        if n + 1 < len(steps):
            total = keep + recv.astype(F32)
            half = total.shape[1] // 2
            keep, send = total[:, :half], total[:, half:].astype(BF16)

    own, *sends = pack(lax.axis_index("grp").reshape(1), keep, recv, groups)
    recvs = [
        lax.ppermute(sent, "grp", [(i, i ^ (t + 1)) for i in range(groups)])
        for t, sent in enumerate(sends)
    ]
    return finish(own, recvs, count // groups)


def solution(mesh):
    return jax.shard_map(
        local,
        mesh=mesh,
        in_specs=(
            P(None, None, "grp", "blk", None),
            P(None, "grp", "blk", None),
            P("grp", "blk", None),
            P("grp", "blk", None),
            P(),
        ),
        out_specs=P(None, "grp", "blk"),
        check_vma=False,
    )
```

time: 132 us -> 68.3 us (0.52)
  waiting for transfers between devices: 69.3 us -> 14.8 us
  Pallas kernels: 0 us -> 20.2 us
  matrix products: 16.1 us -> 0 us
  local copies, waits for them, and re-layouts: 22.5 us -> 7.43 us
  between operations: 13.9 us -> 0.15 us
  starting transfers between devices: 9.23 us -> 18.5 us
  other arithmetic: 0.9 us -> 6.44 us
    reduce_scatter x1 -> x0, waiting for transfers between devices: 45.7 us -> none  [local(): lax.psum_scatter(partial_value, 'blk', scatter_dimension=2, tiled=True)]
    pallas_call x0 -> x4, Pallas kernels: none -> 20.2 us  [the longest x1 11.7 us: tensor_parts(): pl.pallas_call(tensor_kernel, out_shape=[jax.ShapeDtypeStruct((KS, half,...]
    unnamed x3 -> x0, waiting for transfers between devices: 20.2 us -> none
    dot_general x8 -> x0, matrix products: 16.1 us -> none  [local(): lax.dot_general(tested, flat, (((0, 2), (0, 2)), ((), ())), preferred_ele...]
    ppermute x4 -> x10, waiting for transfers between devices: 3.35 us -> 14.8 us  [the longest x3 8.85 us: local(): lax.ppermute(send, 'blk', [(i, i ^ pair[i % 2]) for i in range(blocks)])]
    unnamed x45 -> x9, local copies, waits for them, and re-layouts: 11.6 us -> 2.05 us
    ppermute x4 -> x10, starting transfers between devices: 9 us -> 18.5 us  [the longest x3 6.28 us: local(): lax.ppermute(send, 'blk', [(i, i ^ pair[i % 2]) for i in range(blocks)])]
    another operation x5 -> x0, local copies, waits for them, and re-layouts: 3.16 us -> none  [the longest x1 3.03 us: local(): partial_value = jnp.stack(partials)]
  transfers between devices with their start and end apart: 6 -> 10, of which waited for: 3 -> 5; matrix products, arithmetic and copies ran while one was open for 4% -> 11% of each run, Pallas kernels for 0% -> 7%
where the time goes in v1:
time: 68.3 us; the launch traced here: 67.5 us
  Pallas kernels  20.2 us (30%)
  starting transfers between devices  18.5 us (27%)
  waiting for transfers between devices  14.8 us (22%)
  local copies, waits for them, and re-layouts  7.43 us (11%)
  other arithmetic  6.44 us (9%)
    pallas_call x1, Pallas kernels, tensor_parts(): pl.pallas_call(tensor_kernel, out_shape=[jax.ShapeDtypeStruct((KS, half,...  11.7 us
    ppermute x3, waiting for transfers between devices, local(): lax.ppermute(send, 'blk', [(i, i ^ pair[i % 2]) for i in range(blocks)])  8.85 us
    ppermute x3, starting transfers between devices, local(): lax.ppermute(send, 'blk', [(i, i ^ pair[i % 2]) for i in range(blocks)])  6.28 us
    ppermute x3, waiting for transfers between devices, local(): lax.ppermute(sent, 'grp', [(i, i ^ t + 1) for i in range(groups)])  5.91 us
    ppermute x3, starting transfers between devices, local(): lax.ppermute(sent, 'grp', [(i, i ^ t + 1) for i in range(groups)])  5.23 us
    pallas_call x1, Pallas kernels, relay(): pl.pallas_call(relay_kernel, grid_spec=pltpu.PrefetchScalarGridSpec(num_s...  4.97 us
    ppermute x1, starting transfers between devices, x_halo(): lax.ppermute(slab[:, :, -1:], 'grp', up)  4.49 us
    mul x2, other arithmetic, local(): scale = (0.5 * metric * weight).reshape(comps, cells, nz)  2.06 us
  transfers between devices with their start and end apart: 10, of which 5 were waited for; matrix products, arithmetic and copies ran while one was open for 11% of the time, Pallas kernels for 7%

profile of v1, /device:TPU:0, one launch (start us, length us, event | category | flops | bytes accessed | tf_op | source)
XLA Modules:
  0.0 67.5 jit_solution(1598374561206618708)
XLA Ops:
  0.0 0.9 %fusion.2 = (bf16[3,8,2,1,128]{4,3,2,1,0:T(2,128)(2,1)S(1)}, bf16[3,8,2,1,128]{4,3,2,1,0:T(2,128)(2,1)S(1)}) fusion(bf16[3,256,2,4,128]{4,3,2,1,0:T(4,128)(2,1)} %param.7), kind=kLoop, calls=%fused_computation.25 | loop fusion | bytes 49152 | tf_op jit(solution)/shard_map/slice | solution.py:49
  0.9 0.6 collective-permute-start.3
  1.5 0.7 collective-permute-start.2
  2.2 0.8 %slice_bitcast_fusion.5 = (bf16[3,8,1,4,128]{4,3,1,0,2:T(4,128)(2,1)S(1)}, bf16[1,3,8,1,4,128]{5,4,2,1,3,0:T(4,128)(2,1)S(1)}, bf16[1,3,8,1,4,128]{5,4,2,1,3,0:T(4,128)(2,1)S(1)}, bf16[3,8,1,4,128]{4,3,1,0,2:T(4,128)(2,1)S(1)}) fusion(bf16[3,256,2,4,128]{4,3,2,1,0:T(4,128)(2,1)} %param.7), kind=kLoop, calls=%fused_computation.15 | loop fusion | bytes 147456
  3.0 4.5 %collective-permute-start.1 = (bf16[3,8,1,4,128]{4,3,1,0,2:T(4,128)(2,1)S(1)}, bf16[3,8,1,4,128]{4,3,1,0,2:T(4,128)(2,1)S(1)}, u32[]{:S(2)}, u32[]{:S(2)}) collective-permute-start(bf16[3,8,1,4,128]{4,3,1,0,2:T(4,128)(2,1)S(1)} %get-tuple-element.21), channel_id=1, source_target_pairs={{0,8},{8,16},{16,24},{1,9},{9,17},{17,25},{2,10},{10,18},{18,26},{... | collective-permute-start | bytes 73736 | tf_op jit(solution)/shard_map/ppermute | solution.py:42
  7.4 1.3 %collective-permute-start = (bf16[3,8,1,4,128]{4,3,1,0,2:T(4,128)(2,1)S(1)}, bf16[3,8,1,4,128]{4,3,1,0,2:T(4,128)(2,1)S(1)}, u32[]{:S(2)}, u32[]{:S(2)}) collective-permute-start(bf16[3,8,1,4,128]{4,3,1,0,2:T(4,128)(2,1)S(1)} %get-tuple-element.24), channel_id=1, source_target_pairs={{8,0},{16,8},{24,16},{9,1},{17,9},{25,17},{10,2},{18,10},{26,18},{... | collective-permute-start | bytes 73736 | tf_op jit(solution)/shard_map/ppermute | solution.py:43
  8.7 0.9 %slice_bitcast_fusion = (bf16[1,3,8,2,3,128]{5,4,3,2,1,0:T(4,128)(2,1)S(1)}, bf16[1,3,8,2,3,128]{5,4,3,2,1,0:T(4,128)(2,1)S(1)}) fusion(bf16[3,256,2,4,128]{4,3,2,1,0:T(4,128)(2,1)} %param.7), kind=kLoop, calls=%fused_computation.10 | loop fusion | bytes 147456 | tf_op jit(solution)/shard_map/concatenate | solution.py:257
  9.7 1.0 %fusion.3 = (bf16[3,8,2,4,127]{4,3,2,1,0:T(4,128)(2,1)S(1)}, bf16[3,8,2,4,127]{4,3,2,1,0:T(4,128)(2,1)S(1)}) fusion(bf16[3,256,2,4,128]{4,3,2,1,0:T(4,128)(2,1)} %param.7), kind=kLoop, calls=%fused_computation.26 | loop fusion | bytes 195072 | tf_op jit(solution)/shard_map/slice | solution.py:260
  10.7 1.2 %fusion.1.order_ref = s32[8]{0:T(128)} fusion(s32[8]{0:T(128)} %constant.41.clone, s32[8]{0:T(128)} %constant.42.clone, pred[]{:T(512)S(6)} %eq.32, s32[]{:T(128)S(6)} %axis_index.25), kind=kLoop, calls=%fused_computation.24 | loop fusion | flops 16 | bytes 101 | tf_op jit(solution)/shard_map/xor | solution.py:34
  11.8 0.8 %select_reduce_fusion = f32[2,4,128]{2,1,0:T(4,128)S(1)} fusion(f32[16]{0:T(128)} %param.11, s32[2,4,128]{2,1,0:T(4,128)} %param.9), kind=kLoop, calls=%fused_computation.8 | loop fusion | flops 48128 | bytes 8256 | tf_op jit(solution)/shard_map/reduce_sum | solution.py:59
  12.6 0.8 %fusion = f32[2,4,128]{2,1,0:T(4,128)S(1)} fusion(f32[3,2,4,128]{3,2,1,0:T(4,128)} %param.8, f32[2,4,128]{2,1,0:T(4,128)S(1)} %select_reduce_fusion, s32[2,4,128]{2,1,0:T(4,128)} %param.10), kind=kLoop, calls=%fused_computation.22 | loop fusion | flops 10240 | bytes 24576 | tf_op jit(solution)/shard_map/mul | solution.py:243
  13.4 1.3 %broadcast_multiply_fusion = f32[3,1,8,128]{3,2,1,0:T(8,128)} fusion(f32[3,1,8,128]{3,2,1,0:T(8,128)} %bitcast.36, f32[1,8,128]{2,1,0:T(8,128)S(1)} %bitcast.40), kind=kLoop, calls=%fused_computation.20 | loop fusion | flops 3072 | bytes 28672 | tf_op jit(solution)/shard_map/mul | solution.py:243
  14.7 0.1 convert_subtract_fusion
  14.8 5.0 %relay.1 = (f32[3,8,256,128]{3,2,1,0:T(8,128)}, bf16[256,3072]{1,0:T(8,128)(2,1)}) custom-call(s32[8]{0:T(128)} %fusion.1.order_ref, bf16[3,2048,128]{2,1,0:T(8,128)(2,1)} %bitcast.32), custom_call_target="tpu_custom_call" | custom-call | tf_op jit(solution)/shard_map/relay/pallas_call | solution.py:85
  19.7 0.0 collective-permute-done.3
  19.7 0.0 collective-permute-done.2
  19.8 0.1 convert_subtract_fusion.1
  19.9 0.0 collective-permute-done.1
  19.9 0.0 collective-permute-done
  20.0 0.8 %pad_maximum_fusion.diff_ref = f32[3,24,8,128]{3,2,1,0:T(8,128)} fusion(f32[1,24,8,128]{3,2,1,0:T(8,128)S(1)} %bitcast.33, f32[1,24,8,128]{3,2,1,0:T(8,128)S(1)} %bitcast.34, f32[1,24,8,128]{3,2,1,0:T(8,128)S(1)} %bitcast.35), kind=kLoop, calls=%fused_computation.3 | loop fusion | flops 147456 | bytes 589824 | tf_op jit(solution)/shard_map/stack | solution.py:249
  20.8 11.7 %tensor_parts.1 = (f32[8,128,256]{2,1,0:T(8,128)}, bf16[8,128,256]{2,1,0:T(8,128)(2,1)}) custom-call(f32[3,8,256,128]{3,2,1,0:T(8,128)} %get-tuple-element.13.wide_ref, bf16[256,3072]{1,0:T(8,128)(2,1)} %get-tuple-element.14.adv_ref, f32[3,24,8,128]{3,2,1,0:T(8,128)} %pad_maximum_fusion.diff_ref, f32[3,8,128]{2,1,0:T(8,128)} %bitcast.37), custom_call_target="tpu_custom_call" | custom-call | tf_op jit(solution)/shard_map/tensor_parts/pallas_call | solution.py:153
  32.5 2.6 %collective-permute-start.4 = (bf16[8,128,256]{2,1,0:T(8,128)(2,1)}, bf16[8,128,256]{2,1,0:T(8,128)(2,1)S(1)}, u32[]{:S(2)}, u32[]{:S(2)}) collective-permute-start(bf16[8,128,256]{2,1,0:T(8,128)(2,1)} %get-tuple-element.16), channel_id=1, source_target_pairs={{0,1},{1,0},{2,3},{3,2},{4,5},{5,4},{6,7},{7,6},{8,9},{9,8},{10,11... | collective-permute-start | bytes 1572872 | tf_op jit(solution)/shard_map/ppermute | solution.py:270
  35.1 1.7 %collective-permute-done.4 = bf16[8,128,256]{2,1,0:T(8,128)(2,1)S(1)} collective-permute-done((bf16[8,128,256]{2,1,0:T(8,128)(2,1)}, bf16[8,128,256]{2,1,0:T(8,128)(2,1)S(1)}, u32[]{:S(2)}, u32[]{:S(2)}) %collective-permute-start.4) | collective-permute-done | bytes 524320 | tf_op jit(solution)/shard_map/ppermute | solution.py:270
  36.9 1.3 %convert_add_fusion = f32[8,128,256]{2,1,0:T(8,128)S(1)} fusion(f32[8,128,256]{2,1,0:T(8,128)} %get-tuple-element.15, bf16[8,128,256]{2,1,0:T(8,128)(2,1)S(1)} %collective-permute-done.4), kind=kLoop, calls=%fused_computation | loop fusion | flops 524288 | bytes 2621440 | tf_op jit(solution)/shard_map/add | solution.py:272
  38.2 1.6 %collective-permute-start.5 = (bf16[8,64,256]{2,1,0:T(8,128)(2,1)S(1)}, bf16[8,64,256]{2,1,0:T(8,128)(2,1)S(1)}, u32[]{:S(2)}, u32[]{:S(2)}) collective-permute-start(bf16[8,64,256]{2,1,0:T(8,128)(2,1)S(1)} %slice.95), channel_id=1, source_target_pairs={{0,2},{1,5},{2,0},{3,7},{4,6},{5,1},{6,4},{7,3},{8,10},{9,13},{10,... | collective-permute-start | bytes 786440 | tf_op jit(solution)/shard_map/ppermute | solution.py:270
  39.8 4.9 %collective-permute-done.5 = bf16[8,64,256]{2,1,0:T(8,128)(2,1)S(1)} collective-permute-done((bf16[8,64,256]{2,1,0:T(8,128)(2,1)S(1)}, bf16[8,64,256]{2,1,0:T(8,128)(2,1)S(1)}, u32[]{:S(2)}, u32[]{:S(2)}) %collective-permute-start.5) | collective-permute-done | bytes 262176 | tf_op jit(solution)/shard_map/ppermute | solution.py:270
  44.7 0.1 slice_add_fusion
  44.8 2.2 %collective-permute-start.6 = (bf16[8,32,256]{2,1,0:T(8,128)(2,1)S(1)}, bf16[8,32,256]{2,1,0:T(8,128)(2,1)S(1)}, u32[]{:S(2)}, u32[]{:S(2)}) collective-permute-start(bf16[8,32,256]{2,1,0:T(8,128)(2,1)S(1)} %slice.96), channel_id=1, source_target_pairs={{0,4},{1,3},{2,6},{3,1},{4,0},{5,7},{6,2},{7,5},{8,12},{9,11},{10,... | collective-permute-start | bytes 393224 | tf_op jit(solution)/shard_map/ppermute | solution.py:270
  46.9 0.7 %slice.75.keep_ref = f32[8,32,256]{2,1,0:T(8,128)} slice(f32[8,64,256]{2,1,0:T(8,128)S(1)} %slice_add_fusion), slice={[0:8], [0:32], [0:256]} | slice | bytes 524288 | tf_op jit(solution)/shard_map/slice | solution.py:274
  47.6 2.2 %collective-permute-done.6.recv_ref = bf16[8,32,256]{2,1,0:T(8,128)(2,1)S(1)} collective-permute-done((bf16[8,32,256]{2,1,0:T(8,128)(2,1)S(1)}, bf16[8,32,256]{2,1,0:T(8,128)(2,1)S(1)}, u32[]{:S(2)}, u32[]{:S(2)}) %collective-permute-start.6) | collective-permute-done | bytes 131104 | tf_op jit(solution)/shard_map/ppermute | solution.py:270
  49.9 0.0 copy-start
  49.9 0.7 copy-done
  50.5 1.8 %pack.1 = (f32[4,32,128]{2,1,0:T(8,128)}, bf16[4,32,128]{2,1,0:T(8,128)(2,1)}, bf16[4,32,128]{2,1,0:T(8,128)(2,1)}, bf16[4,32,128]{2,1,0:T(8,128)(2,1)}) custom-call(s32[1]{0:T(128)} %bitcast.me_ref, f32[8,32,256]{2,1,0:T(8,128)} %slice.75.keep_ref, bf16[8,32,256]{2,1,0:T(8,128)(2,1)} %copy-done), custom_call_target="tpu_custom_call" | custom-call | tf_op jit(solution)/shard_map/pack/pallas_call | solution.py:190
  52.3 2.6 %collective-permute-start.7 = (bf16[4,32,128]{2,1,0:T(8,128)(2,1)}, bf16[4,32,128]{2,1,0:T(8,128)(2,1)S(1)}, u32[]{:S(2)}, u32[]{:S(2)}) collective-permute-start(bf16[4,32,128]{2,1,0:T(8,128)(2,1)} %get-tuple-element.18), channel_id=1, source_target_pairs={{0,8},{8,0},{16,24},{24,16},{1,9},{9,1},{17,25},{25,17},{2,10},{10... | collective-permute-start | bytes 98312 | tf_op jit(solution)/shard_map/ppermute | solution.py:278
  55.0 2.6 %collective-permute-start.8 = (bf16[4,32,128]{2,1,0:T(8,128)(2,1)}, bf16[4,32,128]{2,1,0:T(8,128)(2,1)S(1)}, u32[]{:S(2)}, u32[]{:S(2)}) collective-permute-start(bf16[4,32,128]{2,1,0:T(8,128)(2,1)} %get-tuple-element.19), channel_id=1, source_target_pairs={{0,16},{8,24},{16,0},{24,8},{1,17},{9,25},{17,1},{25,9},{2,18},{10... | collective-permute-start | bytes 98312 | tf_op jit(solution)/shard_map/ppermute | solution.py:278
  57.6 0.0 collective-permute-start.9
  57.6 0.0 collective-permute-done.7.rest_0_
  57.6 0.0 copy-start.1
  57.6 3.0 %collective-permute-done.8.rest_1_ = bf16[4,32,128]{2,1,0:T(8,128)(2,1)S(1)} collective-permute-done((bf16[4,32,128]{2,1,0:T(8,128)(2,1)}, bf16[4,32,128]{2,1,0:T(8,128)(2,1)S(1)}, u32[]{:S(2)}, u32[]{:S(2)}) %collective-permute-start.8) | collective-permute-done | bytes 32800 | tf_op jit(solution)/shard_map/ppermute | solution.py:278
  60.6 0.0 copy-start.2
  60.6 2.9 %collective-permute-done.9.rest_2_ = bf16[4,32,128]{2,1,0:T(8,128)(2,1)S(1)} collective-permute-done((bf16[4,32,128]{2,1,0:T(8,128)(2,1)}, bf16[4,32,128]{2,1,0:T(8,128)(2,1)S(1)}, u32[]{:S(2)}, u32[]{:S(2)}) %collective-permute-start.9) | collective-permute-done | bytes 32800 | tf_op jit(solution)/shard_map/ppermute | solution.py:278
  63.5 0.0 copy-start.3
  63.5 0.0 copy-done.1
  63.5 0.0 copy-done.2
  63.5 0.6 copy-done.3
  64.1 1.7 %finish.1 = f32[8,64,32]{2,1,0:T(8,128)} custom-call(f32[4,32,128]{2,1,0:T(8,128)} %get-tuple-element.17.own_ref, bf16[4,32,128]{2,1,0:T(8,128)(2,1)} %copy-done.1, bf16[4,32,128]{2,1,0:T(8,128)(2,1)} %copy-done.2, bf16[4,32,128]{2,1,0:T(8,128)(2,1)} %copy-done.3), custom_call_target="tpu_custom_call" | custom-call | tf_op jit(solution)/shard_map/finish/pallas_call | solution.py:219
  65.8 1.7 %copy.30 = f32[8,64,32]{1,2,0:T(8,128)} copy(f32[8,64,32]{2,1,0:T(8,128)} %finish.1) | data formatting | bytes 131072 | tf_op jit(solution)/shard_map/finish/pallas_call | solution.py:219
  (8 shorter events, 0.2 us)
Async XLA Ops:
  0.9 18.8 %collective-permute-start.3 = (bf16[3,8,2,1,128]{4,1,3,2,0:T(8,128)(2,1)S(1)}, bf16[3,8,2,1,128]{4,1,3,2,0:T(8,128)(2,1)S(1)}, u32[]{:S(2)}, u32[]{:S(2)}) collective-permute-start(bf16[3,8,2,1,128]{4,1,3,2,0:T(8,128)(2,1)S(1)} %get-tuple-element.31), channel_id=1, source_target_pairs={{0,1},{2,3},{4,5},{6,7},{1,0},{3,2},{5,4},{7,6},{8,9},{10,11},{12,... | collective-permute-start | bytes 36872 | tf_op jit(solution)/shard_map/ppermute | solution.py:53
  1.5 18.2 %collective-permute-start.2 = (bf16[3,8,2,1,128]{4,1,3,2,0:T(8,128)(2,1)S(1)}, bf16[3,8,2,1,128]{4,1,3,2,0:T(8,128)(2,1)S(1)}, u32[]{:S(2)}, u32[]{:S(2)}) collective-permute-start(bf16[3,8,2,1,128]{4,1,3,2,0:T(8,128)(2,1)S(1)} %get-tuple-element.32), channel_id=1, source_target_pairs={{1,2},{3,4},{5,6},{2,1},{4,3},{6,5},{9,10},{11,12},{13,14},{10,9},... | collective-permute-start | bytes 36872 | tf_op jit(solution)/shard_map/ppermute | solution.py:52
  3.0 17.0 %collective-permute-start.1 = (bf16[3,8,1,4,128]{4,3,1,0,2:T(4,128)(2,1)S(1)}, bf16[3,8,1,4,128]{4,3,1,0,2:T(4,128)(2,1)S(1)}, u32[]{:S(2)}, u32[]{:S(2)}) collective-permute-start(bf16[3,8,1,4,128]{4,3,1,0,2:T(4,128)(2,1)S(1)} %get-tuple-element.21), channel_id=1, source_target_pairs={{0,8},{8,16},{16,24},{1,9},{9,17},{17,25},{2,10},{10,18},{18,26},{... | collective-permute-start | bytes 73736 | tf_op jit(solution)/shard_map/ppermute | solution.py:42
  7.4 12.5 %collective-permute-start = (bf16[3,8,1,4,128]{4,3,1,0,2:T(4,128)(2,1)S(1)}, bf16[3,8,1,4,128]{4,3,1,0,2:T(4,128)(2,1)S(1)}, u32[]{:S(2)}, u32[]{:S(2)}) collective-permute-start(bf16[3,8,1,4,128]{4,3,1,0,2:T(4,128)(2,1)S(1)} %get-tuple-element.24), channel_id=1, source_target_pairs={{8,0},{16,8},{24,16},{9,1},{17,9},{25,17},{10,2},{18,10},{26,18},{... | collective-permute-start | bytes 73736 | tf_op jit(solution)/shard_map/ppermute | solution.py:43
  32.5 4.3 %collective-permute-start.4 = (bf16[8,128,256]{2,1,0:T(8,128)(2,1)}, bf16[8,128,256]{2,1,0:T(8,128)(2,1)S(1)}, u32[]{:S(2)}, u32[]{:S(2)}) collective-permute-start(bf16[8,128,256]{2,1,0:T(8,128)(2,1)} %get-tuple-element.16), channel_id=1, source_target_pairs={{0,1},{1,0},{2,3},{3,2},{4,5},{5,4},{6,7},{7,6},{8,9},{9,8},{10,11... | collective-permute-start | bytes 1572872 | tf_op jit(solution)/shard_map/ppermute | solution.py:270
  38.2 6.4 %collective-permute-start.5 = (bf16[8,64,256]{2,1,0:T(8,128)(2,1)S(1)}, bf16[8,64,256]{2,1,0:T(8,128)(2,1)S(1)}, u32[]{:S(2)}, u32[]{:S(2)}) collective-permute-start(bf16[8,64,256]{2,1,0:T(8,128)(2,1)S(1)} %slice.95), channel_id=1, source_target_pairs={{0,2},{1,5},{2,0},{3,7},{4,6},{5,1},{6,4},{7,3},{8,10},{9,13},{10,... | collective-permute-start | bytes 786440 | tf_op jit(solution)/shard_map/ppermute | solution.py:270
  44.8 5.1 %collective-permute-start.6 = (bf16[8,32,256]{2,1,0:T(8,128)(2,1)S(1)}, bf16[8,32,256]{2,1,0:T(8,128)(2,1)S(1)}, u32[]{:S(2)}, u32[]{:S(2)}) collective-permute-start(bf16[8,32,256]{2,1,0:T(8,128)(2,1)S(1)} %slice.96), channel_id=1, source_target_pairs={{0,4},{1,3},{2,6},{3,1},{4,0},{5,7},{6,2},{7,5},{8,12},{9,11},{10,... | collective-permute-start | bytes 393224 | tf_op jit(solution)/shard_map/ppermute | solution.py:270
  49.9 0.7 copy-start
  52.3 5.2 %collective-permute-start.7 = (bf16[4,32,128]{2,1,0:T(8,128)(2,1)}, bf16[4,32,128]{2,1,0:T(8,128)(2,1)S(1)}, u32[]{:S(2)}, u32[]{:S(2)}) collective-permute-start(bf16[4,32,128]{2,1,0:T(8,128)(2,1)} %get-tuple-element.18), channel_id=1, source_target_pairs={{0,8},{8,0},{16,24},{24,16},{1,9},{9,1},{17,25},{25,17},{2,10},{10... | collective-permute-start | bytes 98312 | tf_op jit(solution)/shard_map/ppermute | solution.py:278
  55.0 5.6 %collective-permute-start.8 = (bf16[4,32,128]{2,1,0:T(8,128)(2,1)}, bf16[4,32,128]{2,1,0:T(8,128)(2,1)S(1)}, u32[]{:S(2)}, u32[]{:S(2)}) collective-permute-start(bf16[4,32,128]{2,1,0:T(8,128)(2,1)} %get-tuple-element.19), channel_id=1, source_target_pairs={{0,16},{8,24},{16,0},{24,8},{1,17},{9,25},{17,1},{25,9},{2,18},{10... | collective-permute-start | bytes 98312 | tf_op jit(solution)/shard_map/ppermute | solution.py:278
  57.6 5.9 %collective-permute-start.9 = (bf16[4,32,128]{2,1,0:T(8,128)(2,1)}, bf16[4,32,128]{2,1,0:T(8,128)(2,1)S(1)}, u32[]{:S(2)}, u32[]{:S(2)}) collective-permute-start(bf16[4,32,128]{2,1,0:T(8,128)(2,1)} %get-tuple-element.20), channel_id=1, source_target_pairs={{0,24},{8,16},{16,8},{24,0},{1,25},{9,17},{17,9},{25,1},{2,26},{10... | collective-permute-start | bytes 98312 | tf_op jit(solution)/shard_map/ppermute | solution.py:278
  57.6 5.9 %copy-start.1 = (bf16[4,32,128]{2,1,0:T(8,128)(2,1)}, bf16[4,32,128]{2,1,0:T(8,128)(2,1)S(1)}, u32[]{:S(2)}) copy-start(bf16[4,32,128]{2,1,0:T(8,128)(2,1)S(1)} %collective-permute-done.7.rest_0_) | copy-start | bytes 98308
  60.6 2.9 %copy-start.2 = (bf16[4,32,128]{2,1,0:T(8,128)(2,1)}, bf16[4,32,128]{2,1,0:T(8,128)(2,1)S(1)}, u32[]{:S(2)}) copy-start(bf16[4,32,128]{2,1,0:T(8,128)(2,1)S(1)} %collective-permute-done.8.rest_1_) | copy-start | bytes 98308
  63.5 0.6 copy-start.3

commit v2 on v0

v2 whole, which is shorter than its diff:
```python
import jax
import jax.numpy as jnp
import numpy as np
from jax import lax
from jax.experimental import pallas as pl
from jax.experimental.pallas import tpu as pltpu
from jax.sharding import PartitionSpec as P

KS = 8
LANES = 128
TILE = 64
F32 = jnp.float32
BF16 = jnp.bfloat16


def halving_masks(devices, first):
    bits = [1 << b for b in range(first, devices.bit_length() - 1)]
    if first == 0 and len(bits) > 1:
        bits[1] |= 1
    turn = len(bits) // 2
    return [bits, bits[turn:] + bits[:turn]]


def xor_table(masks):
    table = [0]
    for mask in reversed(masks):
        table = table + [t ^ mask for t in table]
    return table


def adv_order(blocks, me, odd):
    even_masks, odd_masks = halving_masks(blocks, 1)
    near, far = xor_table(even_masks), xor_table(odd_masks)
    tables = jnp.asarray([near + [t ^ 1 for t in far], far + [t ^ 1 for t in near]], jnp.int32)
    return me ^ jnp.where(odd, tables[1], tables[0])


def test_order(groups, me, odd):
    tables = jnp.asarray([xor_table(m) for m in halving_masks(groups, 0)], jnp.int32)
    return me ^ jnp.where(odd, tables[1], tables[0])


def vmem(shape, dtype):
    return pltpu.VMEM(shape, dtype)


def inside(x):
    return pltpu.with_memory_space_constraint(x, pltpu.VMEM)


def relay_kernel(order_ref, region_ref, rows_ref, metric_ref, map_ref, flag_ref, norm, wide_ref, adv_ref,
                 scale_ref, in_ref, flat_ref, sem):
    comps, cells, count, _ = wide_ref.shape
    blocks = order_ref.shape[0]
    width = count // blocks
    copies = [
        pltpu.make_async_copy(rows_ref.at[c], in_ref.at[c], sem.at[c]) for c in range(comps)
    ]
    for copy in copies:
        copy.start()
    scale = jnp.zeros(map_ref.shape, F32)
    for label in range(region_ref.shape[0]):
        scale = jnp.where(map_ref[...] == label, region_ref[label], scale)
    flags = flag_ref[...]
    fluid = jnp.where(flags == 0, 1.0, jnp.where(flags == 1, 0.0, 0.5))
    weight = scale * fluid * norm / (metric_ref[0] * metric_ref[1] * metric_ref[2])
    for d in range(comps):
        scale_ref[d] = 0.5 * metric_ref[d] * weight
    for c in range(comps):
        copies[c].wait()
        flat_ref[c] = in_ref[c].astype(F32)
        for r in range(cells):
            wide_ref[c, r] = flat_ref[c, pl.ds(r, count, stride=cells), :]
        for p in range(blocks):
            start = pl.multiple_of(order_ref[p] * width, width)
            for r in range(cells):
                part = wide_ref[c, r, pl.ds(start, width), :]
                col = (c * cells + r) * LANES
                adv_ref[p * width : (p + 1) * width, col : col + LANES] = part.astype(BF16)


def relay(order, region_scale, rows, metric, block_map, flags, norm, count):
    comps, total, _ = rows.shape
    cells = total // count
    smem = pl.BlockSpec(memory_space=pltpu.SMEM)
    whole = pl.BlockSpec(memory_space=pltpu.VMEM)
    return pl.pallas_call(
        lambda *refs: relay_kernel(*refs[:6], norm, *refs[6:]),
        in_specs=[smem, smem, pl.BlockSpec(memory_space=pl.ANY), whole, whole, whole],
        out_shape=[
            vmem((comps, cells, count, LANES), F32),
            vmem((count, comps * cells * LANES), BF16),
            vmem((comps, cells, LANES), F32),
        ],
        scratch_shapes=[
            pltpu.VMEM((comps, total, LANES), BF16),
            pltpu.VMEM((comps, total, LANES), F32),
            pltpu.SemaphoreType.DMA((comps,)),
        ],
        compiler_params=pltpu.CompilerParams(vmem_limit_bytes=16 << 20),
        name="relay",
    )(order, region_scale, rows, metric, block_map, flags)


def tensor_kernel(order_ref, edge_ref, wide_ref, adv_ref, scale_ref, slab_ref, down_ref, up_ref, near_ref,
                  far_ref, swap, ny, keep_ref, send_ref, grad_ref, t0_ref, t1_ref):
    comps, cells, count, _ = wide_ref.shape
    half = keep_ref.shape[1]
    chunks = order_ref.shape[0]
    width = count // chunks
    tile = min(width, TILE)
    odd = edge_ref[4] == 1
    row = lax.broadcasted_iota(jnp.int32, (cells, LANES), 0)
    lane = lax.broadcasted_iota(jnp.int32, (cells, LANES), 1)
    ends = [edge_ref[e] == 1 for e in range(4)]

    def shift_in(own, before, after, by, axis, first, last, no_before, no_after):
        size = own.shape[axis]
        prev = pltpu.roll(own, by, axis)
        succ = pltpu.roll(own, size - by, axis)
        if before is not None:
            before = jnp.where(no_before, 0.0, pltpu.roll(before, first[1], 0) if first[1] else before)
            after = jnp.where(no_after, 0.0, pltpu.roll(after, last[1], 0) if last[1] else after)
        else:
            before = after = 0.0
        return jnp.where(last[0], after, succ) - jnp.where(first[0], before, prev)

    for c in range(comps):
        for k in range(KS):
            at = pl.ds(k * cells, cells)
            own, down, up, near, far = (
                ref[c, at, :].astype(F32) for ref in (slab_ref, down_ref, up_ref, near_ref, far_ref)
            )
            left, right = jnp.where(odd, near, far), jnp.where(odd, far, near)
            shift_x = ny % cells
            diffs = [
                shift_in(own, down, up, ny % cells, 0, (row < ny, shift_x), (row >= cells - ny, shift_x),
                         ends[0], ends[1]),
                shift_in(own, left, right, 1, 0, (row % ny == 0, (cells - ny + 1) % cells),
                         (row % ny == ny - 1, (ny - 1) % cells), ends[2], ends[3]),
                shift_in(own, None, None, 1, 1, (lane == 0, 0), (lane == LANES - 1, 0), None, None),
            ]
            for d in range(comps):
                grad_ref[(k * comps + d) * comps + c] = diffs[d] * scale_ref[d]

    def build(k, t_ref):
        for q in range(chunks):
            base = pl.multiple_of(order_ref[q] * width, width)
            for r in range(cells):
                for i in range(0, width, tile):
                    a = [wide_ref[c, r, pl.ds(base + i, tile), :] for c in range(comps)]
                    for d in range(comps):
                        at = (k * comps + d) * comps
                        g = [grad_ref[at + c, pl.ds(r, 1), :] for c in range(comps)]
                        total = a[0] * g[0]
                        for c in range(1, comps):
                            total = total + a[c] * g[c]
                        col = (d * cells + r) * LANES
                        top = q * width + i
                        t_ref[top : top + tile, col : col + LANES] = total.astype(BF16)

    def contract(k, t_ref):
        out = lax.dot_general(
            adv_ref[...], t_ref[...], (((1,), (1,)), ((), ())), preferred_element_type=F32
        )
        keep_ref[k] = out[:half]
        gone = out[half:]
        send_ref[k] = jnp.concatenate(
            [gone[:, s * width : (s + 1) * width] for s in swap], axis=1
        ).astype(BF16)

    build(0, t0_ref)

    def step(n, carry):
        build(2 * n + 1, t1_ref)
        contract(2 * n, t0_ref)
        build(2 * n + 2, t0_ref)
        contract(2 * n + 1, t1_ref)
        return carry

    lax.fori_loop(0, KS // 2 - 1, step, 0)
    build(KS - 1, t1_ref)
    contract(KS - 2, t0_ref)
    contract(KS - 1, t1_ref)


def tensor_parts(order, edges, wide, adv, scale, slabs, swap, ny):
    comps, cells, count, _ = wide.shape
    half = count // 2
    depth = adv.shape[1]
    smem = pl.BlockSpec(memory_space=pltpu.SMEM)
    whole = pl.BlockSpec(memory_space=pltpu.VMEM)
    return pl.pallas_call(
        lambda *refs: tensor_kernel(*refs[:10], swap, ny, *refs[10:]),
        in_specs=[smem, smem] + [whole] * 8,
        out_shape=[vmem((KS, half, count), F32), vmem((KS, half, count), BF16)],
        scratch_shapes=[
            pltpu.VMEM((KS * comps * comps, cells, LANES), F32),
            pltpu.VMEM((count, depth), BF16),
            pltpu.VMEM((count, depth), BF16),
        ],
        compiler_params=pltpu.CompilerParams(vmem_limit_bytes=16 << 20),
        name="tensor_parts",
    )(order, edges, *(inside(x) for x in (wide, adv, scale, *slabs)))


def fold_parts(rows, group, side):
    half = group // 2
    first = side * half
    parts = [r[:, g + first : g + first + half] for r in rows for g in range(0, rows[0].shape[1], group)]
    return parts[0] if len(parts) == 1 else jnp.concatenate(parts, axis=1)


def fold(keep, recv, group):
    count, rows, lanes = keep.shape
    shape = (count // 2, rows, lanes)

    def kernel(keep_ref, recv_ref, own_ref, send_ref):
        for n in range(count // 2):
            pair = [keep_ref[m] + recv_ref[m].astype(F32) for m in (2 * n, 2 * n + 1)]
            own_ref[n] = fold_parts(pair, group, 0)
            send_ref[n] = fold_parts(pair, group, 1).astype(BF16)

    return pl.pallas_call(
        kernel,
        out_shape=[vmem(shape, F32), vmem(shape, BF16)],
        compiler_params=pltpu.CompilerParams(vmem_limit_bytes=4 << 20),
        name="fold",
    )(inside(keep), inside(recv))


def finish(keep, recv, width):
    count, rows, lanes = keep.shape
    pieces = lanes // width

    def kernel(keep_ref, recv_ref, out_ref):
        for n in range(count):
            total = keep_ref[n] + recv_ref[n].astype(F32)
            for q in range(pieces):
                out_ref[n * pieces + q] = total[:, q * width : (q + 1) * width]

    return pl.pallas_call(
        kernel,
        out_shape=jax.ShapeDtypeStruct((KS, rows, width), F32),
        compiler_params=pltpu.CompilerParams(vmem_limit_bytes=4 << 20),
        name="finish",
    )(inside(keep), inside(recv))


def exchange(send, axis, masks):
    count = lax.axis_size(axis)
    return lax.ppermute(send, axis, [(i, i ^ masks[i % 2]) for i in range(count)])


def local(modes, metric, block_map, flags, region_scale):
    groups = lax.axis_size("grp")
    blocks = lax.axis_size("blk")
    comps, count, nx, ny, nz = modes.shape
    cells = nx * ny
    total_cells = nx * groups * ny * blocks * nz
    norm = float(total_cells) ** (-0.5)
    block, layer = lax.axis_index("blk"), lax.axis_index("grp")
    odd = block % 2 == 1

    rows = modes.reshape(comps, count * cells, nz)
    slab = rows[:, : KS * cells]
    ring = range(groups)
    down = lax.ppermute(slab, "grp", [(i, (i + 1) % groups) for i in ring])
    up = lax.ppermute(slab, "grp", [((i + 1) % groups, i) for i in ring])
    turn = [(i + 1) % blocks if i % 2 else (i - 1) % blocks for i in range(blocks)]
    far = lax.ppermute(slab, "blk", list(enumerate(turn)))
    near = lax.ppermute(slab, "blk", [(i, i ^ 1) for i in range(blocks)])

    wide, adv, scale = relay(
        adv_order(blocks, block, odd),
        region_scale,
        rows,
        metric.reshape(comps, cells, nz),
        block_map.reshape(cells, nz),
        flags.reshape(cells, nz),
        norm,
        count,
    )
    edges = jnp.stack([layer == 0, layer == groups - 1, block == 0, block == blocks - 1, odd])
    even_masks, odd_masks = halving_masks(groups, 0)
    even_order = xor_table(even_masks)
    swap = [even_order.index(t) for t in xor_table(odd_masks)]
    keep, send = tensor_parts(
        test_order(groups, layer, odd),
        edges.astype(jnp.int32),
        wide,
        adv,
        scale,
        (slab, down, up, near, far),
        swap,
        ny,
    )

    recv = exchange(send, "blk", [1, 1])
    for masks in zip(*halving_masks(blocks, 1)):
        total = keep + recv.astype(F32)
        half = total.shape[1] // 2
        keep, send = total[:, :half], total[:, half:].astype(BF16)
        recv = exchange(send, "blk", masks)
    width = count
    for masks in zip(even_masks, odd_masks):
        if width > LANES:
            total = keep + recv.astype(F32)
            half = width // 2
            keep, send = total[..., :half], total[..., half:].astype(BF16)
        else:
            keep, send = fold(keep, recv, width)
        width //= 2
        pairs = [
            (g * blocks + b, (g ^ masks[b % 2]) * blocks + b)
            for g in range(groups)
            for b in range(blocks)
        ]
        recv = lax.ppermute(send, ("grp", "blk"), pairs)
    return jnp.swapaxes(finish(keep, recv, width), 1, 2)


def solution(mesh):
    return jax.shard_map(
        local,
        mesh=mesh,
        in_specs=(
            P(None, None, "grp", "blk", None),
            P(None, "grp", "blk", None),
            P("grp", "blk", None),
            P("grp", "blk", None),
            P(),
        ),
        out_specs=P(None, "grp", "blk"),
        check_vma=False,
    )
```

time: 132 us -> 49.7 us (0.38)
  waiting for transfers between devices: 69.3 us -> 16.7 us
  local copies, waits for them, and re-layouts: 22.5 us -> 5.12 us
  matrix products: 16.1 us -> 0 us
  between operations: 13.9 us -> 0.12 us
  Pallas kernels: 0 us -> 12.1 us
  starting transfers between devices: 9.23 us -> 13.8 us
    reduce_scatter x1 -> x0, waiting for transfers between devices: 45.7 us -> none  [local(): lax.psum_scatter(partial_value, 'blk', scatter_dimension=2, tiled=True)]
    unnamed x3 -> x0, waiting for transfers between devices: 20.2 us -> none
    dot_general x8 -> x0, matrix products: 16.1 us -> none  [local(): lax.dot_general(tested, flat, (((0, 2), (0, 2)), ((), ())), preferred_ele...]
    ppermute x4 -> x9, waiting for transfers between devices: 3.35 us -> 16.7 us  [the longest x3 10.6 us: exchange(): lax.ppermute(send, axis, [(i, i ^ masks[i % 2]) for i in range(count)])]
    pallas_call x0 -> x4, Pallas kernels: none -> 12.1 us  [the longest x1 9.61 us: tensor_parts(): pl.pallas_call(lambda *refs: tensor_kernel(*refs[:10], swap, ny, *refs[10...]
    unnamed x45 -> x10, local copies, waits for them, and re-layouts: 11.6 us -> 4.14 us
    ppermute x4 -> x9, starting transfers between devices: 9 us -> 13.8 us  [the longest x2 3.96 us: local(): recv = lax.ppermute(send, ('grp', 'blk'), pairs)]
    another operation x5 -> x1, local copies, waits for them, and re-layouts: 3.16 us -> 0.1 us  [local(): jnp.stack([layer == 0, layer == groups - 1, block == 0, block == blocks -...]
  transfers between devices with their start and end apart: 6 -> 9, of which waited for: 3 -> 5; matrix products, arithmetic and copies ran while one was open for 4% -> 3% of each run, Pallas kernels for 0% -> 3%
where the time goes in v2:
time: 49.7 us; the launch traced here: 49.4 us
  waiting for transfers between devices  16.7 us (34%)
  starting transfers between devices  13.8 us (28%)
  Pallas kernels  12.1 us (24%)
  local copies, waits for them, and re-layouts  5.12 us (10%)
  other arithmetic  1.54 us (3%)
    ppermute x3, waiting for transfers between devices, exchange(): lax.ppermute(send, axis, [(i, i ^ masks[i % 2]) for i in range(count)])  10.6 us
    pallas_call x1, Pallas kernels, tensor_parts(): pl.pallas_call(lambda *refs: tensor_kernel(*refs[:10], swap, ny, *refs[10...  9.61 us
    ppermute x2, waiting for transfers between devices, local(): recv = lax.ppermute(send, ('grp', 'blk'), pairs)  6.13 us
    unnamed x10, local copies, waits for them, and re-layouts  4.14 us
    ppermute x2, starting transfers between devices, local(): recv = lax.ppermute(send, ('grp', 'blk'), pairs)  3.96 us
    ppermute x1, starting transfers between devices, local(): up = lax.ppermute(slab, 'grp', [((i + 1) % groups, i) for i in ring])  3.6 us
    ppermute x1, starting transfers between devices, local(): far = lax.ppermute(slab, 'blk', list(enumerate(turn)))  3.36 us
    ppermute x3, starting transfers between devices, exchange(): lax.ppermute(send, axis, [(i, i ^ masks[i % 2]) for i in range(count)])  2.88 us
  transfers between devices with their start and end apart: 9, of which 5 were waited for; matrix products, arithmetic and copies ran while one was open for 3% of the time, Pallas kernels for 3%

profile of v2, /device:TPU:0, one launch (start us, length us, event | category | flops | bytes accessed | tf_op | source)
XLA Modules:
  0.0 49.4 jit_solution(6273050865269475016)
XLA Ops:
  0.0 0.8 %slice.47.refs_5_ = bf16[3,64,128]{2,1,0:T(8,128)(2,1)S(1)} slice(bf16[3,2048,128]{2,1,0:T(8,128)(2,1)} %bitcast.14), slice={[0:3], [0:64], [0:128]} | slice | bytes 98304 | tf_op jit(solution)/shard_map/slice | solution.py:266
  0.8 3.4 %collective-permute-start.3 = (bf16[3,64,128]{2,1,0:T(8,128)(2,1)S(1)}, bf16[3,64,128]{2,1,0:T(8,128)(2,1)S(1)}, u32[]{:S(2)}, u32[]{:S(2)}) collective-permute-start(bf16[3,64,128]{2,1,0:T(8,128)(2,1)S(1)} %slice.47.refs_5_), channel_id=1, source_target_pairs={{0,7},{1,2},{2,1},{3,4},{4,3},{5,6},{6,5},{7,0},{8,15},{9,10},{10,... | collective-permute-start | bytes 147464 | tf_op jit(solution)/shard_map/ppermute | solution.py:271
  4.2 0.0 collective-permute-start.2
  4.2 3.6 %collective-permute-start.1 = (bf16[3,64,128]{2,1,0:T(8,128)(2,1)S(1)}, bf16[3,64,128]{2,1,0:T(8,128)(2,1)S(1)}, u32[]{:S(2)}, u32[]{:S(2)}) collective-permute-start(bf16[3,64,128]{2,1,0:T(8,128)(2,1)S(1)} %slice.47.refs_5_), channel_id=1, source_target_pairs={{8,0},{16,8},{24,16},{0,24},{9,1},{17,9},{25,17},{1,25},{10,2},{18... | collective-permute-start | bytes 147464 | tf_op jit(solution)/shard_map/ppermute | solution.py:269
  7.8 0.0 collective-permute-start
  7.8 0.7 %fusion.3.refs_0_ = s32[8]{0:T(128)S(1)} fusion(s32[1,8]{1,0:T(1,128)} %constant.39, s32[1,8]{1,0:T(1,128)} %constant.40, pred[]{:T(512)} %eq.17, s32[]{:T(128)S(6)} %axis_index.25), kind=kLoop, calls=%fused_computation.11 | loop fusion | flops 16 | bytes 101 | tf_op jit(solution)/shard_map/xor | solution.py:35
  8.4 0.7 %fusion.1.refs_0_ = s32[4]{0:T(128)S(1)} fusion(s32[1,4]{1,0:T(1,128)} %constant.37, s32[1,4]{1,0:T(1,128)} %constant.38, pred[]{:T(512)} %eq.17, s32[]{:T(128)S(6)} %axis_index.23), kind=kLoop, calls=%fused_computation.9 | loop fusion | flops 8 | bytes 53 | tf_op jit(solution)/shard_map/xor | solution.py:40
  9.1 0.1 stack.23
  9.2 0.0 copy-start
  9.2 1.4 %copy-done = bf16[3,256,2,4,128]{4,3,2,1,0:T(4,128)(2,1)S(1)} copy-done((bf16[3,256,2,4,128]{4,3,2,1,0:T(4,128)(2,1)S(1)}, bf16[3,256,2,4,128]{4,3,2,1,0:T(4,128)(2,1)}, u32[]{:S(2)}) %copy-start) | copy-done | bytes 1572888
  10.6 0.0 copy-start.1
  10.6 0.7 %copy-done.1 = f32[3,2,4,128]{3,2,1,0:T(4,128)S(1)} copy-done((f32[3,2,4,128]{3,2,1,0:T(4,128)S(1)}, f32[3,2,4,128]{3,2,1,0:T(4,128)}, u32[]{:S(2)}) %copy-start.1) | copy-done | bytes 12312
  11.3 0.0 copy-start.2
  11.3 0.7 %copy-done.2 = s32[2,4,128]{2,1,0:T(4,128)S(1)} copy-done((s32[2,4,128]{2,1,0:T(4,128)S(1)}, s32[2,4,128]{2,1,0:T(4,128)}, u32[]{:S(2)}) %copy-start.2) | copy-done | bytes 4120
  12.0 0.0 copy-start.3
  12.0 0.7 %copy-done.3 = s32[2,4,128]{2,1,0:T(4,128)S(1)} copy-done((s32[2,4,128]{2,1,0:T(4,128)S(1)}, s32[2,4,128]{2,1,0:T(4,128)}, u32[]{:S(2)}) %copy-start.3) | copy-done | bytes 4120
  12.7 0.0 copy-start.4
  12.7 0.7 %copy-done.4 = f32[16]{0:T(128)S(1)} copy-done((f32[16]{0:T(128)S(1)}, f32[16]{0:T(128)}, u32[]{:S(2)}) %copy-start.4) | copy-done | bytes 88
  13.4 1.7 %relay.1 = (f32[3,8,256,128]{3,2,1,0:T(8,128)S(1)}, bf16[256,3072]{1,0:T(8,128)(2,1)S(1)}, f32[3,8,128]{2,1,0:T(8,128)S(1)}) custom-call(s32[8]{0:T(128)S(1)} %fusion.3.refs_0_, f32[16]{0:T(128)S(1)} %copy-done.4, bf16[3,2048,128]{2,1,0:T(8,128)(2,1)S(1)} %bitcast.15, f32[3,8,128]{2,1,0:T(8,128)S(1)} %bitcast.16, s32[8,128]{1,0:T(8,128)S(1)} %bitcast.17, ...), custom_call_target="tpu_custom_call" | custom-call | tf_op jit(solution)/shard_map/relay/pallas_call | solution.py:87
  15.0 0.0 collective-permute-done.3.refs_9_
  15.0 0.0 collective-permute-done.2.refs_8_
  15.0 0.0 collective-permute-done.1.refs_7_
  15.1 0.0 collective-permute-done.refs_6_
  15.1 9.6 %tensor_parts.1 = (f32[8,128,256]{2,1,0:T(8,128)S(1)}, bf16[8,128,256]{2,1,0:T(8,128)(2,1)S(1)}) custom-call(s32[4]{0:T(128)S(1)} %fusion.1.refs_0_, s32[5]{0:T(128)S(1)} %convert_element_type.15.refs_1_, f32[3,8,256,128]{3,2,1,0:T(8,128)S(1)} %get-tuple-element.12.refs_2_, bf16[256,3072]{1,0:T(8,128)(2,1)S(1)} %get-tuple-element.13.refs_3_, ...), custom_call_target="tpu_custom_call" | custom-call | tf_op jit(solution)/shard_map/tensor_parts/pallas_call | solution.py:193
  24.7 0.3 collective-permute-start.4
  25.0 1.7 %collective-permute-done.4 = bf16[8,128,256]{2,1,0:T(8,128)(2,1)S(1)} collective-permute-done((bf16[8,128,256]{2,1,0:T(8,128)(2,1)S(1)}, bf16[8,128,256]{2,1,0:T(8,128)(2,1)S(1)}, u32[]{:S(2)}, u32[]{:S(2)}) %collective-permute-start.4) | collective-permute-done | bytes 524320 | tf_op jit(solution)/shard_map/ppermute | solution.py:252
  26.7 0.1 convert_add_fusion
  26.8 1.3 %collective-permute-start.5 = (bf16[8,64,256]{2,1,0:T(8,128)(2,1)S(1)}, bf16[8,64,256]{2,1,0:T(8,128)(2,1)S(1)}, u32[]{:S(2)}, u32[]{:S(2)}) collective-permute-start(bf16[8,64,256]{2,1,0:T(8,128)(2,1)S(1)} %slice.59), channel_id=1, source_target_pairs={{0,2},{1,5},{2,0},{3,7},{4,6},{5,1},{6,4},{7,3},{8,10},{9,13},{10,... | collective-permute-start | bytes 786440 | tf_op jit(solution)/shard_map/ppermute | solution.py:252
  28.1 5.2 %collective-permute-done.5 = bf16[8,64,256]{2,1,0:T(8,128)(2,1)S(1)} collective-permute-done((bf16[8,64,256]{2,1,0:T(8,128)(2,1)S(1)}, bf16[8,64,256]{2,1,0:T(8,128)(2,1)S(1)}, u32[]{:S(2)}, u32[]{:S(2)}) %collective-permute-start.5) | collective-permute-done | bytes 262176 | tf_op jit(solution)/shard_map/ppermute | solution.py:252
  33.3 0.1 slice_add_fusion
  33.4 1.3 %collective-permute-start.6 = (bf16[8,32,256]{2,1,0:T(8,128)(2,1)S(1)}, bf16[8,32,256]{2,1,0:T(8,128)(2,1)S(1)}, u32[]{:S(2)}, u32[]{:S(2)}) collective-permute-start(bf16[8,32,256]{2,1,0:T(8,128)(2,1)S(1)} %slice.60), channel_id=1, source_target_pairs={{0,4},{1,3},{2,6},{3,1},{4,0},{5,7},{6,2},{7,5},{8,12},{9,11},{10,... | collective-permute-start | bytes 393224 | tf_op jit(solution)/shard_map/ppermute | solution.py:252
  34.7 3.7 %collective-permute-done.6 = bf16[8,32,256]{2,1,0:T(8,128)(2,1)S(1)} collective-permute-done((bf16[8,32,256]{2,1,0:T(8,128)(2,1)S(1)}, bf16[8,32,256]{2,1,0:T(8,128)(2,1)S(1)}, u32[]{:S(2)}, u32[]{:S(2)}) %collective-permute-start.6) | collective-permute-done | bytes 131104 | tf_op jit(solution)/shard_map/ppermute | solution.py:252
  38.4 0.1 collective-permute-start.7
  38.5 4.2 %collective-permute-done.7.recv_ref = bf16[8,32,128]{2,1,0:T(8,128)(2,1)S(1)} collective-permute-done((bf16[8,32,128]{2,1,0:T(8,128)(2,1)S(1)}, bf16[8,32,128]{2,1,0:T(8,128)(2,1)S(1)}, u32[]{:S(2)}, u32[]{:S(2)}) %collective-permute-start.7) | collective-permute-done | bytes 65568 | tf_op jit(solution)/shard_map/ppermute | solution.py:319
  42.8 0.1 fold.1
  42.9 3.9 %collective-permute-start.8 = (bf16[4,32,128]{2,1,0:T(8,128)(2,1)S(1)}, bf16[4,32,128]{2,1,0:T(8,128)(2,1)S(1)}, u32[]{:S(2)}, u32[]{:S(2)}) collective-permute-start(bf16[4,32,128]{2,1,0:T(8,128)(2,1)S(1)} %get-tuple-element.18), channel_id=1, source_target_pairs={{0,24},{1,9},{2,26},{3,11},{4,28},{5,13},{6,30},{7,15},{8,16},{9,1... | collective-permute-start | bytes 98312 | tf_op jit(solution)/shard_map/ppermute | solution.py:319
  46.8 1.9 %collective-permute-done.8.recv_ref = bf16[4,32,128]{2,1,0:T(8,128)(2,1)S(1)} collective-permute-done((bf16[4,32,128]{2,1,0:T(8,128)(2,1)S(1)}, bf16[4,32,128]{2,1,0:T(8,128)(2,1)S(1)}, u32[]{:S(2)}, u32[]{:S(2)}) %collective-permute-start.8) | collective-permute-done | bytes 32800 | tf_op jit(solution)/shard_map/ppermute | solution.py:319
  48.7 0.7 %finish.1 = f32[8,32,64]{2,1,0:T(8,128)} custom-call(f32[4,32,128]{2,1,0:T(8,128)S(1)} %get-tuple-element.17.keep_ref, bf16[4,32,128]{2,1,0:T(8,128)(2,1)S(1)} %collective-permute-done.8.recv_ref), custom_call_target="tpu_custom_call" | custom-call | tf_op jit(solution)/shard_map/finish/pallas_call | solution.py:242
  (6 shorter events, 0.1 us)
Async XLA Ops:
  0.8 14.2 %collective-permute-start.3 = (bf16[3,64,128]{2,1,0:T(8,128)(2,1)S(1)}, bf16[3,64,128]{2,1,0:T(8,128)(2,1)S(1)}, u32[]{:S(2)}, u32[]{:S(2)}) collective-permute-start(bf16[3,64,128]{2,1,0:T(8,128)(2,1)S(1)} %slice.47.refs_5_), channel_id=1, source_target_pairs={{0,7},{1,2},{2,1},{3,4},{4,3},{5,6},{6,5},{7,0},{8,15},{9,10},{10,... | collective-permute-start | bytes 147464 | tf_op jit(solution)/shard_map/ppermute | solution.py:271
  4.2 10.9 %collective-permute-start.2 = (bf16[3,64,128]{2,1,0:T(8,128)(2,1)S(1)}, bf16[3,64,128]{2,1,0:T(8,128)(2,1)S(1)}, u32[]{:S(2)}, u32[]{:S(2)}) collective-permute-start(bf16[3,64,128]{2,1,0:T(8,128)(2,1)S(1)} %slice.47.refs_5_), channel_id=1, source_target_pairs={{0,1},{1,0},{2,3},{3,2},{4,5},{5,4},{6,7},{7,6},{8,9},{9,8},{10,11... | collective-permute-start | bytes 147464 | tf_op jit(solution)/shard_map/ppermute | solution.py:272
  4.2 10.9 %collective-permute-start.1 = (bf16[3,64,128]{2,1,0:T(8,128)(2,1)S(1)}, bf16[3,64,128]{2,1,0:T(8,128)(2,1)S(1)}, u32[]{:S(2)}, u32[]{:S(2)}) collective-permute-start(bf16[3,64,128]{2,1,0:T(8,128)(2,1)S(1)} %slice.47.refs_5_), channel_id=1, source_target_pairs={{8,0},{16,8},{24,16},{0,24},{9,1},{17,9},{25,17},{1,25},{10,2},{18... | collective-permute-start | bytes 147464 | tf_op jit(solution)/shard_map/ppermute | solution.py:269
  7.8 7.3 %collective-permute-start = (bf16[3,64,128]{2,1,0:T(8,128)(2,1)S(1)}, bf16[3,64,128]{2,1,0:T(8,128)(2,1)S(1)}, u32[]{:S(2)}, u32[]{:S(2)}) collective-permute-start(bf16[3,64,128]{2,1,0:T(8,128)(2,1)S(1)} %slice.47.refs_5_), channel_id=1, source_target_pairs={{0,8},{8,16},{16,24},{24,0},{1,9},{9,17},{17,25},{25,1},{2,10},{10... | collective-permute-start | bytes 147464 | tf_op jit(solution)/shard_map/ppermute | solution.py:268
  9.2 1.4 %copy-start = (bf16[3,256,2,4,128]{4,3,2,1,0:T(4,128)(2,1)S(1)}, bf16[3,256,2,4,128]{4,3,2,1,0:T(4,128)(2,1)}, u32[]{:S(2)}) copy-start(bf16[3,256,2,4,128]{4,3,2,1,0:T(4,128)(2,1)} %param.7) | copy-start | bytes 4718596
  10.6 0.7 %copy-start.1 = (f32[3,2,4,128]{3,2,1,0:T(4,128)S(1)}, f32[3,2,4,128]{3,2,1,0:T(4,128)}, u32[]{:S(2)}) copy-start(f32[3,2,4,128]{3,2,1,0:T(4,128)} %param.8) | copy-start | bytes 36868
  11.3 0.7 %copy-start.2 = (s32[2,4,128]{2,1,0:T(4,128)S(1)}, s32[2,4,128]{2,1,0:T(4,128)}, u32[]{:S(2)}) copy-start(s32[2,4,128]{2,1,0:T(4,128)} %param.9) | copy-start | bytes 12292
  12.0 0.7 %copy-start.3 = (s32[2,4,128]{2,1,0:T(4,128)S(1)}, s32[2,4,128]{2,1,0:T(4,128)}, u32[]{:S(2)}) copy-start(s32[2,4,128]{2,1,0:T(4,128)} %param.10) | copy-start | bytes 12292
  12.7 0.7 %copy-start.4 = (f32[16]{0:T(128)S(1)}, f32[16]{0:T(128)}, u32[]{:S(2)}) copy-start(f32[16]{0:T(128)} %refs_1_.1) | copy-start | bytes 196
  24.7 2.0 %collective-permute-start.4 = (bf16[8,128,256]{2,1,0:T(8,128)(2,1)S(1)}, bf16[8,128,256]{2,1,0:T(8,128)(2,1)S(1)}, u32[]{:S(2)}, u32[]{:S(2)}) collective-permute-start(bf16[8,128,256]{2,1,0:T(8,128)(2,1)S(1)} %get-tuple-element.16), channel_id=1, source_target_pairs={{0,1},{1,0},{2,3},{3,2},{4,5},{5,4},{6,7},{7,6},{8,9},{9,8},{10,11... | collective-permute-start | bytes 1572872 | tf_op jit(solution)/shard_map/ppermute | solution.py:252
  26.8 6.4 %collective-permute-start.5 = (bf16[8,64,256]{2,1,0:T(8,128)(2,1)S(1)}, bf16[8,64,256]{2,1,0:T(8,128)(2,1)S(1)}, u32[]{:S(2)}, u32[]{:S(2)}) collective-permute-start(bf16[8,64,256]{2,1,0:T(8,128)(2,1)S(1)} %slice.59), channel_id=1, source_target_pairs={{0,2},{1,5},{2,0},{3,7},{4,6},{5,1},{6,4},{7,3},{8,10},{9,13},{10,... | collective-permute-start | bytes 786440 | tf_op jit(solution)/shard_map/ppermute | solution.py:252
  33.4 5.0 %collective-permute-start.6 = (bf16[8,32,256]{2,1,0:T(8,128)(2,1)S(1)}, bf16[8,32,256]{2,1,0:T(8,128)(2,1)S(1)}, u32[]{:S(2)}, u32[]{:S(2)}) collective-permute-start(bf16[8,32,256]{2,1,0:T(8,128)(2,1)S(1)} %slice.60), channel_id=1, source_target_pairs={{0,4},{1,3},{2,6},{3,1},{4,0},{5,7},{6,2},{7,5},{8,12},{9,11},{10,... | collective-permute-start | bytes 393224 | tf_op jit(solution)/shard_map/ppermute | solution.py:252
  38.4 4.3 %collective-permute-start.7 = (bf16[8,32,128]{2,1,0:T(8,128)(2,1)S(1)}, bf16[8,32,128]{2,1,0:T(8,128)(2,1)S(1)}, u32[]{:S(2)}, u32[]{:S(2)}) collective-permute-start(bf16[8,32,128]{2,1,0:T(8,128)(2,1)S(1)} %slice.61), channel_id=1, source_target_pairs={{0,8},{1,25},{2,10},{3,27},{4,12},{5,29},{6,14},{7,31},{8,0},{9,17... | collective-permute-start | bytes 196616 | tf_op jit(solution)/shard_map/ppermute | solution.py:319
  42.9 5.8 %collective-permute-start.8 = (bf16[4,32,128]{2,1,0:T(8,128)(2,1)S(1)}, bf16[4,32,128]{2,1,0:T(8,128)(2,1)S(1)}, u32[]{:S(2)}, u32[]{:S(2)}) collective-permute-start(bf16[4,32,128]{2,1,0:T(8,128)(2,1)S(1)} %get-tuple-element.18), channel_id=1, source_target_pairs={{0,24},{1,9},{2,26},{3,11},{4,28},{5,13},{6,30},{7,15},{8,16},{9,1... | collective-permute-start | bytes 98312 | tf_op jit(solution)/shard_map/ppermute | solution.py:319

commit v3 on v2

--- a/solution.py
+++ b/solution.py
@@ -15,8 +15,6 @@
 
 def halving_masks(devices, first):
     bits = [1 << b for b in range(first, devices.bit_length() - 1)]
-    if first == 0 and len(bits) > 1:
-        bits[1] |= 1
     turn = len(bits) // 2
     return [bits, bits[turn:] + bits[:turn]]
 
@@ -28,16 +26,23 @@
     return table
 
 
-def adv_order(blocks, me, odd):
-    even_masks, odd_masks = halving_masks(blocks, 1)
-    near, far = xor_table(even_masks), xor_table(odd_masks)
-    tables = jnp.asarray([near + [t ^ 1 for t in far], far + [t ^ 1 for t in near]], jnp.int32)
-    return me ^ jnp.where(odd, tables[1], tables[0])
-
-
-def test_order(groups, me, odd):
-    tables = jnp.asarray([xor_table(m) for m in halving_masks(groups, 0)], jnp.int32)
-    return me ^ jnp.where(odd, tables[1], tables[0])
+def place():
+    block, layer = lax.axis_index("blk"), lax.axis_index("grp")
+    return block, layer, block % 2 == 1
+
+
+def adv_order(blocks):
+    block, _, odd = place()
+    near, far = (xor_table(masks) for masks in halving_masks(blocks, 1))
+    even = near + [t ^ 1 for t in far]
+    other = far + [t ^ 1 for t in near]
+    return [block ^ (e if e == o else jnp.where(odd, o, e)) for e, o in zip(even, other)]
+
+
+def test_order(groups):
+    _, layer, odd = place()
+    even, other = (xor_table(masks) for masks in halving_masks(groups, 0))
+    return [layer ^ (e if e == o else jnp.where(odd, o, e)) for e, o in zip(even, other)]
 
 
 def vmem(shape, dtype):
@@ -48,16 +53,28 @@
     return pltpu.with_memory_space_constraint(x, pltpu.VMEM)
 
 
-def relay_kernel(order_ref, region_ref, rows_ref, metric_ref, map_ref, flag_ref, norm, wide_ref, adv_ref,
-                 scale_ref, in_ref, flat_ref, sem):
+def relay_kernel(region_in, rows_in, metric_in, map_in, flag_in, norm, blocks, wide_ref, adv_ref,
+                 scale_ref, region_ref, rows_ref, metric_ref, map_ref, flag_ref, flat_ref, sem):
     comps, cells, count, _ = wide_ref.shape
-    blocks = order_ref.shape[0]
     width = count // blocks
-    copies = [
-        pltpu.make_async_copy(rows_ref.at[c], in_ref.at[c], sem.at[c]) for c in range(comps)
-    ]
-    for copy in copies:
+    pairs = [(region_in, region_ref), (metric_in, metric_ref), (map_in, map_ref), (flag_in, flag_ref)]
+    pairs += [(rows_in.at[c], rows_ref.at[c]) for c in range(comps)]
+    copies = [pltpu.make_async_copy(a, b, sem.at[n]) for n, (a, b) in enumerate(pairs)]
+    for copy in copies[4:] + copies[:4]:
         copy.start()
+    order = adv_order(blocks)
+    for c in range(comps):
+        copies[4 + c].wait()
+        flat_ref[c] = rows_ref[c].astype(F32)
+        for r in range(cells):
+            wide_ref[c, r] = flat_ref[c, pl.ds(r, count, stride=cells), :]
+        for p in range(blocks):
+            start = pl.multiple_of(order[p] * width, width)
+            for r in range(cells):
+                part = wide_ref[c, r, pl.ds(start, width), :]
+                adv_ref[c * cells + r, p * width : (p + 1) * width, :] = part.astype(BF16)
+    for copy in copies[:4]:
+        copy.wait()
     scale = jnp.zeros(map_ref.shape, F32)
     for label in range(region_ref.shape[0]):
         scale = jnp.where(map_ref[...] == label, region_ref[label], scale)
@@ -66,53 +83,47 @@
     weight = scale * fluid * norm / (metric_ref[0] * metric_ref[1] * metric_ref[2])
     for d in range(comps):
         scale_ref[d] = 0.5 * metric_ref[d] * weight
-    for c in range(comps):
-        copies[c].wait()
-        flat_ref[c] = in_ref[c].astype(F32)
-        for r in range(cells):
-            wide_ref[c, r] = flat_ref[c, pl.ds(r, count, stride=cells), :]
-        for p in range(blocks):
-            start = pl.multiple_of(order_ref[p] * width, width)
-            for r in range(cells):
-                part = wide_ref[c, r, pl.ds(start, width), :]
-                col = (c * cells + r) * LANES
-                adv_ref[p * width : (p + 1) * width, col : col + LANES] = part.astype(BF16)
-
-
-def relay(order, region_scale, rows, metric, block_map, flags, norm, count):
+
+
+def relay(region_scale, rows, metric, block_map, flags, norm, count, blocks):
     comps, total, _ = rows.shape
     cells = total // count
-    smem = pl.BlockSpec(memory_space=pltpu.SMEM)
-    whole = pl.BlockSpec(memory_space=pltpu.VMEM)
     return pl.pallas_call(
-        lambda *refs: relay_kernel(*refs[:6], norm, *refs[6:]),
-        in_specs=[smem, smem, pl.BlockSpec(memory_space=pl.ANY), whole, whole, whole],
+        lambda *refs: relay_kernel(*refs[:5], norm, blocks, *refs[5:]),
+        in_specs=[pl.BlockSpec(memory_space=pltpu.HBM)] * 5,
         out_shape=[
             vmem((comps, cells, count, LANES), F32),
-            vmem((count, comps * cells * LANES), BF16),
+            vmem((comps * cells, count, LANES), BF16),
             vmem((comps, cells, LANES), F32),
         ],
         scratch_shapes=[
-            pltpu.VMEM((comps, total, LANES), BF16),
+            pltpu.SMEM(region_scale.shape, F32),
+            pltpu.VMEM(rows.shape, BF16),
+            pltpu.VMEM(metric.shape, F32),
+            pltpu.VMEM(block_map.shape, jnp.int32),
+            pltpu.VMEM(flags.shape, jnp.int32),
             pltpu.VMEM((comps, total, LANES), F32),
-            pltpu.SemaphoreType.DMA((comps,)),
+            pltpu.SemaphoreType.DMA((4 + comps,)),
         ],
         compiler_params=pltpu.CompilerParams(vmem_limit_bytes=16 << 20),
         name="relay",
-    )(order, region_scale, rows, metric, block_map, flags)
-
-
-def tensor_kernel(order_ref, edge_ref, wide_ref, adv_ref, scale_ref, slab_ref, down_ref, up_ref, near_ref,
-                  far_ref, swap, ny, keep_ref, send_ref, grad_ref, t0_ref, t1_ref):
+    )(*(
+        pltpu.with_memory_space_constraint(x, pltpu.HBM)
+        for x in (region_scale, rows, metric, block_map, flags)
+    ))
+
+
+def tensor_kernel(wide_ref, adv_ref, scale_ref, slab_ref, down_ref, up_ref, near_ref,
+                  far_ref, swap, ny, groups, blocks, keep_ref, send_ref, grad_ref, t0_ref, t1_ref):
     comps, cells, count, _ = wide_ref.shape
     half = keep_ref.shape[1]
-    chunks = order_ref.shape[0]
-    width = count // chunks
+    width = count // groups
     tile = min(width, TILE)
-    odd = edge_ref[4] == 1
+    order = test_order(groups)
+    block, layer, odd = place()
     row = lax.broadcasted_iota(jnp.int32, (cells, LANES), 0)
     lane = lax.broadcasted_iota(jnp.int32, (cells, LANES), 1)
-    ends = [edge_ref[e] == 1 for e in range(4)]
+    ends = [layer == 0, layer == groups - 1, block == 0, block == blocks - 1]
 
     def shift_in(own, before, after, by, axis, first, last, no_before, no_after):
         size = own.shape[axis]
@@ -144,8 +155,8 @@
                 grad_ref[(k * comps + d) * comps + c] = diffs[d] * scale_ref[d]
 
     def build(k, t_ref):
-        for q in range(chunks):
-            base = pl.multiple_of(order_ref[q] * width, width)
+        for q in range(groups):
+            base = pl.multiple_of(order[q] * width, width)
             for r in range(cells):
                 for i in range(0, width, tile):
                     a = [wide_ref[c, r, pl.ds(base + i, tile), :] for c in range(comps)]
@@ -155,13 +166,15 @@
                         total = a[0] * g[0]
                         for c in range(1, comps):
                             total = total + a[c] * g[c]
-                        col = (d * cells + r) * LANES
                         top = q * width + i
-                        t_ref[top : top + tile, col : col + LANES] = total.astype(BF16)
+                        t_ref[d * cells + r, top : top + tile, :] = total.astype(BF16)
 
     def contract(k, t_ref):
+        adv, tested = (
+            jnp.concatenate([ref[n] for n in range(ref.shape[0])], axis=1) for ref in (adv_ref, t_ref)
+        )
         out = lax.dot_general(
-            adv_ref[...], t_ref[...], (((1,), (1,)), ((), ())), preferred_element_type=F32
+            adv, tested, (((1,), (1,)), ((), ())), preferred_element_type=F32
         )
         keep_ref[k] = out[:half]
         gone = out[half:]
@@ -184,24 +197,20 @@
     contract(KS - 1, t1_ref)
 
 
-def tensor_parts(order, edges, wide, adv, scale, slabs, swap, ny):
+def tensor_parts(wide, adv, scale, slabs, swap, ny, groups, blocks):
     comps, cells, count, _ = wide.shape
     half = count // 2
-    depth = adv.shape[1]
-    smem = pl.BlockSpec(memory_space=pltpu.SMEM)
-    whole = pl.BlockSpec(memory_space=pltpu.VMEM)
     return pl.pallas_call(
-        lambda *refs: tensor_kernel(*refs[:10], swap, ny, *refs[10:]),
-        in_specs=[smem, smem] + [whole] * 8,
+        lambda *refs: tensor_kernel(*refs[:8], swap, ny, groups, blocks, *refs[8:]),
         out_shape=[vmem((KS, half, count), F32), vmem((KS, half, count), BF16)],
         scratch_shapes=[
             pltpu.VMEM((KS * comps * comps, cells, LANES), F32),
-            pltpu.VMEM((count, depth), BF16),
-            pltpu.VMEM((count, depth), BF16),
+            pltpu.VMEM(adv.shape, BF16),
+            pltpu.VMEM(adv.shape, BF16),
         ],
         compiler_params=pltpu.CompilerParams(vmem_limit_bytes=16 << 20),
         name="tensor_parts",
-    )(order, edges, *(inside(x) for x in (wide, adv, scale, *slabs)))
+    )(*(inside(x) for x in (wide, adv, scale, *slabs)))
 
 
 def fold_parts(rows, group, side):
@@ -259,8 +268,6 @@
     cells = nx * ny
     total_cells = nx * groups * ny * blocks * nz
     norm = float(total_cells) ** (-0.5)
-    block, layer = lax.axis_index("blk"), lax.axis_index("grp")
-    odd = block % 2 == 1
 
     rows = modes.reshape(comps, count * cells, nz)
     slab = rows[:, : KS * cells]
@@ -272,7 +279,6 @@
     near = lax.ppermute(slab, "blk", [(i, i ^ 1) for i in range(blocks)])
 
     wide, adv, scale = relay(
-        adv_order(blocks, block, odd),
         region_scale,
         rows,
         metric.reshape(comps, cells, nz),
@@ -280,20 +286,20 @@
         flags.reshape(cells, nz),
         norm,
         count,
+        blocks,
     )
-    edges = jnp.stack([layer == 0, layer == groups - 1, block == 0, block == blocks - 1, odd])
     even_masks, odd_masks = halving_masks(groups, 0)
     even_order = xor_table(even_masks)
     swap = [even_order.index(t) for t in xor_table(odd_masks)]
     keep, send = tensor_parts(
-        test_order(groups, layer, odd),
-        edges.astype(jnp.int32),
         wide,
         adv,
         scale,
         (slab, down, up, near, far),
         swap,
         ny,
+        groups,
+        blocks,
     )
 
     recv = exchange(send, "blk", [1, 1])

time: 49.7 us -> 45 us (0.905)
  waiting for transfers between devices: 16.7 us -> 23.6 us
  local copies, waits for them, and re-layouts: 5.12 us -> 0.87 us
  starting transfers between devices: 13.8 us -> 9.76 us
  Pallas kernels: 12.1 us -> 10.3 us
  other arithmetic: 1.54 us -> 0.21 us
    unnamed x10 -> x0, local copies, waits for them, and re-layouts: 4.14 us -> none
    ppermute x2, starting transfers between devices: 3.96 us -> 0.14 us  [local(): recv = lax.ppermute(send, ('grp', 'blk'), pairs)]
    ppermute x1, waiting for transfers between devices: 0.01 us -> 3.75 us  [local(): down = lax.ppermute(slab, 'grp', [(i, (i + 1) % groups) for i in ring])]
    ppermute x2, waiting for transfers between devices: 6.13 us -> 9.03 us  [local(): recv = lax.ppermute(send, ('grp', 'blk'), pairs)]
    pallas_call x2, Pallas kernels: 11.3 us -> 9.42 us  [the longest x1 7.38 us: tensor_parts(): pl.pallas_call(lambda *refs: tensor_kernel(*refs[:8], swap, ny, groups, b...]
    xor x2 -> x0, other arithmetic: 1.32 us -> none  [the longest x1 0.66 us: adv_order(): return me ^ jnp.where(odd, tables[1], tables[0])]
  transfers between devices with their start and end apart: 9 -> 9, of which waited for: 5 -> 7; matrix products, arithmetic and copies ran while one was open for 3% -> 0% of each run, Pallas kernels for 3% -> 5%
where the time goes in v3:
time: 45 us; the launch traced here: 44.8 us
  waiting for transfers between devices  23.6 us (52%)
  Pallas kernels  10.3 us (23%)
  starting transfers between devices  9.76 us (22%)
  local copies, waits for them, and re-layouts  0.87 us (2%)
    ppermute x3, waiting for transfers between devices, exchange(): lax.ppermute(send, axis, [(i, i ^ masks[i % 2]) for i in range(count)])  10.8 us
    ppermute x2, waiting for transfers between devices, local(): recv = lax.ppermute(send, ('grp', 'blk'), pairs)  9.03 us
    pallas_call x1, Pallas kernels, tensor_parts(): pl.pallas_call(lambda *refs: tensor_kernel(*refs[:8], swap, ny, groups, b...  7.38 us
    ppermute x1, waiting for transfers between devices, local(): down = lax.ppermute(slab, 'grp', [(i, (i + 1) % groups) for i in ring])  3.75 us
    ppermute x1, starting transfers between devices, local(): up = lax.ppermute(slab, 'grp', [((i + 1) % groups, i) for i in ring])  3.6 us
    ppermute x1, starting transfers between devices, local(): far = lax.ppermute(slab, 'blk', list(enumerate(turn)))  3.36 us
    ppermute x3, starting transfers between devices, exchange(): lax.ppermute(send, axis, [(i, i ^ masks[i % 2]) for i in range(count)])  2.65 us
    pallas_call x1, Pallas kernels, relay(): pl.pallas_call(lambda *refs: relay_kernel(*refs[:5], norm, blocks, *refs[...  2.04 us
  transfers between devices with their start and end apart: 9, of which 7 were waited for; matrix products, arithmetic and copies ran while one was open for 0% of the time, Pallas kernels for 5%

profile of v3, /device:TPU:0, one launch (start us, length us, event | category | flops | bytes accessed | tf_op | source)
XLA Modules:
  0.0 44.8 jit_solution(7665856786730459964)
XLA Ops:
  0.0 0.8 %slice.31.refs_3_ = bf16[3,64,128]{2,1,0:T(8,128)(2,1)S(1)} slice(bf16[3,2048,128]{2,1,0:T(8,128)(2,1)} %bitcast.5), slice={[0:3], [0:64], [0:128]} | slice | bytes 98304 | tf_op jit(solution)/shard_map/slice | solution.py:273
  0.8 3.4 %collective-permute-start.3 = (bf16[3,64,128]{2,1,0:T(8,128)(2,1)S(1)}, bf16[3,64,128]{2,1,0:T(8,128)(2,1)S(1)}, u32[]{:S(2)}, u32[]{:S(2)}) collective-permute-start(bf16[3,64,128]{2,1,0:T(8,128)(2,1)S(1)} %slice.31.refs_3_), channel_id=1, source_target_pairs={{0,7},{1,2},{2,1},{3,4},{4,3},{5,6},{6,5},{7,0},{8,15},{9,10},{10,... | collective-permute-start | bytes 147464 | tf_op jit(solution)/shard_map/ppermute | solution.py:278
  4.2 0.0 collective-permute-start.2
  4.2 3.6 %collective-permute-start.1 = (bf16[3,64,128]{2,1,0:T(8,128)(2,1)S(1)}, bf16[3,64,128]{2,1,0:T(8,128)(2,1)S(1)}, u32[]{:S(2)}, u32[]{:S(2)}) collective-permute-start(bf16[3,64,128]{2,1,0:T(8,128)(2,1)S(1)} %slice.31.refs_3_), channel_id=1, source_target_pairs={{8,0},{16,8},{24,16},{0,24},{9,1},{17,9},{25,17},{1,25},{10,2},{18... | collective-permute-start | bytes 147464 | tf_op jit(solution)/shard_map/ppermute | solution.py:276
  7.8 0.0 collective-permute-start
  7.8 2.0 %relay.1 = (f32[3,8,256,128]{3,2,1,0:T(8,128)S(1)}, bf16[24,256,128]{2,1,0:T(8,128)(2,1)S(1)}, f32[3,8,128]{2,1,0:T(8,128)S(1)}) custom-call(f32[16]{0:T(128)} %refs_0_.1, bf16[3,2048,128]{2,1,0:T(8,128)(2,1)} %bitcast.6, f32[3,8,128]{2,1,0:T(8,128)} %bitcast.7, s32[8,128]{1,0:T(8,128)} %bitcast.8, s32[8,128]{1,0:T(8,128)} %bitcast.9), custom_call_target="tpu_custom_call" | custom-call | tf_op jit(solution)/shard_map/relay/pallas_call | solution.py:91
  9.8 0.0 collective-permute-done.3.refs_7_
  9.8 0.0 collective-permute-done.2.refs_6_
  9.8 0.1 collective-permute-done.1.refs_5_
  9.9 3.8 %collective-permute-done.refs_4_ = bf16[3,64,128]{2,1,0:T(8,128)(2,1)S(1)} collective-permute-done((bf16[3,64,128]{2,1,0:T(8,128)(2,1)S(1)}, bf16[3,64,128]{2,1,0:T(8,128)(2,1)S(1)}, u32[]{:S(2)}, u32[]{:S(2)}) %collective-permute-start) | collective-permute-done | bytes 49184 | tf_op jit(solution)/shard_map/ppermute | solution.py:275
  13.7 7.4 %tensor_parts.1 = (f32[8,128,256]{2,1,0:T(8,128)S(1)}, bf16[8,128,256]{2,1,0:T(8,128)(2,1)S(1)}) custom-call(f32[3,8,256,128]{3,2,1,0:T(8,128)S(1)} %get-tuple-element.12.refs_0_, bf16[24,256,128]{2,1,0:T(8,128)(2,1)S(1)} %get-tuple-element.13.refs_1_, f32[3,8,128]{2,1,0:T(8,128)S(1)} %get-tuple-element.14.refs_2_, bf16[3,64,128]{2,1,0:T(8,128)(2,1)S(1)} %slice.31.refs_3_, ...), custom_call_target="tpu_custom_call" | custom-call | tf_op jit(solution)/shard_map/tensor_parts/pallas_call | solution.py:203
  21.0 0.1 collective-permute-start.4
  21.1 1.9 %collective-permute-done.4 = bf16[8,128,256]{2,1,0:T(8,128)(2,1)S(1)} collective-permute-done((bf16[8,128,256]{2,1,0:T(8,128)(2,1)S(1)}, bf16[8,128,256]{2,1,0:T(8,128)(2,1)S(1)}, u32[]{:S(2)}, u32[]{:S(2)}) %collective-permute-start.4) | collective-permute-done | bytes 524320 | tf_op jit(solution)/shard_map/ppermute | solution.py:261
  23.0 0.1 convert_add_fusion
  23.2 1.3 %collective-permute-start.5 = (bf16[8,64,256]{2,1,0:T(8,128)(2,1)S(1)}, bf16[8,64,256]{2,1,0:T(8,128)(2,1)S(1)}, u32[]{:S(2)}, u32[]{:S(2)}) collective-permute-start(bf16[8,64,256]{2,1,0:T(8,128)(2,1)S(1)} %slice.43), channel_id=1, source_target_pairs={{0,2},{1,5},{2,0},{3,7},{4,6},{5,1},{6,4},{7,3},{8,10},{9,13},{10,... | collective-permute-start | bytes 786440 | tf_op jit(solution)/shard_map/ppermute | solution.py:261
  24.5 5.2 %collective-permute-done.5 = bf16[8,64,256]{2,1,0:T(8,128)(2,1)S(1)} collective-permute-done((bf16[8,64,256]{2,1,0:T(8,128)(2,1)S(1)}, bf16[8,64,256]{2,1,0:T(8,128)(2,1)S(1)}, u32[]{:S(2)}, u32[]{:S(2)}) %collective-permute-start.5) | collective-permute-done | bytes 262176 | tf_op jit(solution)/shard_map/ppermute | solution.py:261
  29.6 0.1 slice_add_fusion
  29.7 1.3 %collective-permute-start.6 = (bf16[8,32,256]{2,1,0:T(8,128)(2,1)S(1)}, bf16[8,32,256]{2,1,0:T(8,128)(2,1)S(1)}, u32[]{:S(2)}, u32[]{:S(2)}) collective-permute-start(bf16[8,32,256]{2,1,0:T(8,128)(2,1)S(1)} %slice.44), channel_id=1, source_target_pairs={{0,4},{1,3},{2,6},{3,1},{4,0},{5,7},{6,2},{7,5},{8,12},{9,11},{10,... | collective-permute-start | bytes 393224 | tf_op jit(solution)/shard_map/ppermute | solution.py:261
  31.0 3.7 %collective-permute-done.6 = bf16[8,32,256]{2,1,0:T(8,128)(2,1)S(1)} collective-permute-done((bf16[8,32,256]{2,1,0:T(8,128)(2,1)S(1)}, bf16[8,32,256]{2,1,0:T(8,128)(2,1)S(1)}, u32[]{:S(2)}, u32[]{:S(2)}) %collective-permute-start.6) | collective-permute-done | bytes 131104 | tf_op jit(solution)/shard_map/ppermute | solution.py:261
  34.8 0.1 collective-permute-start.7
  34.9 4.2 %collective-permute-done.7.recv_ref = bf16[8,32,128]{2,1,0:T(8,128)(2,1)S(1)} collective-permute-done((bf16[8,32,128]{2,1,0:T(8,128)(2,1)S(1)}, bf16[8,32,128]{2,1,0:T(8,128)(2,1)S(1)}, u32[]{:S(2)}, u32[]{:S(2)}) %collective-permute-start.7) | collective-permute-done | bytes 65568 | tf_op jit(solution)/shard_map/ppermute | solution.py:325
  39.1 0.1 fold.1
  39.2 0.1 collective-permute-start.8
  39.3 4.8 %collective-permute-done.8.recv_ref = bf16[4,32,128]{2,1,0:T(8,128)(2,1)S(1)} collective-permute-done((bf16[4,32,128]{2,1,0:T(8,128)(2,1)S(1)}, bf16[4,32,128]{2,1,0:T(8,128)(2,1)S(1)}, u32[]{:S(2)}, u32[]{:S(2)}) %collective-permute-start.8) | collective-permute-done | bytes 32800 | tf_op jit(solution)/shard_map/ppermute | solution.py:325
  44.1 0.7 %finish.1 = f32[8,32,64]{2,1,0:T(8,128)} custom-call(f32[4,32,128]{2,1,0:T(8,128)S(1)} %get-tuple-element.17.keep_ref, bf16[4,32,128]{2,1,0:T(8,128)(2,1)S(1)} %collective-permute-done.8.recv_ref), custom_call_target="tpu_custom_call" | custom-call | tf_op jit(solution)/shard_map/finish/pallas_call | solution.py:251
  (5 shorter events, 0.1 us)
Async XLA Ops:
  0.8 9.0 %collective-permute-start.3 = (bf16[3,64,128]{2,1,0:T(8,128)(2,1)S(1)}, bf16[3,64,128]{2,1,0:T(8,128)(2,1)S(1)}, u32[]{:S(2)}, u32[]{:S(2)}) collective-permute-start(bf16[3,64,128]{2,1,0:T(8,128)(2,1)S(1)} %slice.31.refs_3_), channel_id=1, source_target_pairs={{0,7},{1,2},{2,1},{3,4},{4,3},{5,6},{6,5},{7,0},{8,15},{9,10},{10,... | collective-permute-start | bytes 147464 | tf_op jit(solution)/shard_map/ppermute | solution.py:278
  4.2 5.7 %collective-permute-start.2 = (bf16[3,64,128]{2,1,0:T(8,128)(2,1)S(1)}, bf16[3,64,128]{2,1,0:T(8,128)(2,1)S(1)}, u32[]{:S(2)}, u32[]{:S(2)}) collective-permute-start(bf16[3,64,128]{2,1,0:T(8,128)(2,1)S(1)} %slice.31.refs_3_), channel_id=1, source_target_pairs={{0,1},{1,0},{2,3},{3,2},{4,5},{5,4},{6,7},{7,6},{8,9},{9,8},{10,11... | collective-permute-start | bytes 147464 | tf_op jit(solution)/shard_map/ppermute | solution.py:279
  4.2 5.7 %collective-permute-start.1 = (bf16[3,64,128]{2,1,0:T(8,128)(2,1)S(1)}, bf16[3,64,128]{2,1,0:T(8,128)(2,1)S(1)}, u32[]{:S(2)}, u32[]{:S(2)}) collective-permute-start(bf16[3,64,128]{2,1,0:T(8,128)(2,1)S(1)} %slice.31.refs_3_), channel_id=1, source_target_pairs={{8,0},{16,8},{24,16},{0,24},{9,1},{17,9},{25,17},{1,25},{10,2},{18... | collective-permute-start | bytes 147464 | tf_op jit(solution)/shard_map/ppermute | solution.py:276
  7.8 5.9 %collective-permute-start = (bf16[3,64,128]{2,1,0:T(8,128)(2,1)S(1)}, bf16[3,64,128]{2,1,0:T(8,128)(2,1)S(1)}, u32[]{:S(2)}, u32[]{:S(2)}) collective-permute-start(bf16[3,64,128]{2,1,0:T(8,128)(2,1)S(1)} %slice.31.refs_3_), channel_id=1, source_target_pairs={{0,8},{8,16},{16,24},{24,0},{1,9},{9,17},{17,25},{25,1},{2,10},{10... | collective-permute-start | bytes 147464 | tf_op jit(solution)/shard_map/ppermute | solution.py:275
  21.0 2.0 %collective-permute-start.4 = (bf16[8,128,256]{2,1,0:T(8,128)(2,1)S(1)}, bf16[8,128,256]{2,1,0:T(8,128)(2,1)S(1)}, u32[]{:S(2)}, u32[]{:S(2)}) collective-permute-start(bf16[8,128,256]{2,1,0:T(8,128)(2,1)S(1)} %get-tuple-element.16), channel_id=1, source_target_pairs={{0,1},{1,0},{2,3},{3,2},{4,5},{5,4},{6,7},{7,6},{8,9},{9,8},{10,11... | collective-permute-start | bytes 1572872 | tf_op jit(solution)/shard_map/ppermute | solution.py:261
  23.2 6.4 %collective-permute-start.5 = (bf16[8,64,256]{2,1,0:T(8,128)(2,1)S(1)}, bf16[8,64,256]{2,1,0:T(8,128)(2,1)S(1)}, u32[]{:S(2)}, u32[]{:S(2)}) collective-permute-start(bf16[8,64,256]{2,1,0:T(8,128)(2,1)S(1)} %slice.43), channel_id=1, source_target_pairs={{0,2},{1,5},{2,0},{3,7},{4,6},{5,1},{6,4},{7,3},{8,10},{9,13},{10,... | collective-permute-start | bytes 786440 | tf_op jit(solution)/shard_map/ppermute | solution.py:261
  29.7 5.0 %collective-permute-start.6 = (bf16[8,32,256]{2,1,0:T(8,128)(2,1)S(1)}, bf16[8,32,256]{2,1,0:T(8,128)(2,1)S(1)}, u32[]{:S(2)}, u32[]{:S(2)}) collective-permute-start(bf16[8,32,256]{2,1,0:T(8,128)(2,1)S(1)} %slice.44), channel_id=1, source_target_pairs={{0,4},{1,3},{2,6},{3,1},{4,0},{5,7},{6,2},{7,5},{8,12},{9,11},{10,... | collective-permute-start | bytes 393224 | tf_op jit(solution)/shard_map/ppermute | solution.py:261
  34.8 4.3 %collective-permute-start.7 = (bf16[8,32,128]{2,1,0:T(8,128)(2,1)S(1)}, bf16[8,32,128]{2,1,0:T(8,128)(2,1)S(1)}, u32[]{:S(2)}, u32[]{:S(2)}) collective-permute-start(bf16[8,32,128]{2,1,0:T(8,128)(2,1)S(1)} %slice.45), channel_id=1, source_target_pairs={{0,8},{1,17},{2,10},{3,19},{4,12},{5,21},{6,14},{7,23},{8,0},{9,25... | collective-permute-start | bytes 196616 | tf_op jit(solution)/shard_map/ppermute | solution.py:325
  39.2 4.9 %collective-permute-start.8 = (bf16[4,32,128]{2,1,0:T(8,128)(2,1)S(1)}, bf16[4,32,128]{2,1,0:T(8,128)(2,1)S(1)}, u32[]{:S(2)}, u32[]{:S(2)}) collective-permute-start(bf16[4,32,128]{2,1,0:T(8,128)(2,1)S(1)} %get-tuple-element.18), channel_id=1, source_target_pairs={{0,16},{1,9},{2,18},{3,11},{4,20},{5,13},{6,22},{7,15},{8,24},{9,1... | collective-permute-start | bytes 98312 | tf_op jit(solution)/shard_map/ppermute | solution.py:325

commit v4 on v3

--- a/solution.py
+++ b/solution.py
@@ -113,7 +113,7 @@
     ))
 
 
-def tensor_kernel(wide_ref, adv_ref, scale_ref, slab_ref, down_ref, up_ref, near_ref,
+def tensor_kernel(wide_ref, adv_ref, scale_ref, slab_ref, inner_ref, outer_ref, near_ref,
                   far_ref, swap, ny, groups, blocks, keep_ref, send_ref, grad_ref, t0_ref, t1_ref):
     comps, cells, count, _ = wide_ref.shape
     half = keep_ref.shape[1]
@@ -121,6 +121,7 @@
     tile = min(width, TILE)
     order = test_order(groups)
     block, layer, odd = place()
+    raised = layer % 2 == 1
     row = lax.broadcasted_iota(jnp.int32, (cells, LANES), 0)
     lane = lax.broadcasted_iota(jnp.int32, (cells, LANES), 1)
     ends = [layer == 0, layer == groups - 1, block == 0, block == blocks - 1]
@@ -139,9 +140,11 @@
     for c in range(comps):
         for k in range(KS):
             at = pl.ds(k * cells, cells)
-            own, down, up, near, far = (
-                ref[c, at, :].astype(F32) for ref in (slab_ref, down_ref, up_ref, near_ref, far_ref)
+            own, inner, outer, near, far = (
+                ref[c, at, :].astype(F32)
+                for ref in (slab_ref, inner_ref, outer_ref, near_ref, far_ref)
             )
+            down, up = jnp.where(raised, inner, outer), jnp.where(raised, outer, inner)
             left, right = jnp.where(odd, near, far), jnp.where(odd, far, near)
             shift_x = ny % cells
             diffs = [
@@ -271,9 +274,10 @@
 
     rows = modes.reshape(comps, count * cells, nz)
     slab = rows[:, : KS * cells]
-    ring = range(groups)
-    down = lax.ppermute(slab, "grp", [(i, (i + 1) % groups) for i in ring])
-    up = lax.ppermute(slab, "grp", [((i + 1) % groups, i) for i in ring])
+    inner = lax.ppermute(slab, "grp", [(i, i ^ 1) for i in range(groups)])
+    outer = lax.ppermute(
+        slab, "grp", [(i, i + 1 if i % 2 else i - 1) for i in range(1, groups - 1)]
+    )
     turn = [(i + 1) % blocks if i % 2 else (i - 1) % blocks for i in range(blocks)]
     far = lax.ppermute(slab, "blk", list(enumerate(turn)))
     near = lax.ppermute(slab, "blk", [(i, i ^ 1) for i in range(blocks)])
@@ -295,7 +299,7 @@
         wide,
         adv,
         scale,
-        (slab, down, up, near, far),
+        (slab, inner, outer, near, far),
         swap,
         ny,
         groups,

time: 45 us -> 42.8 us (0.951)
  waiting for transfers between devices: 23.6 us -> 16.2 us
  starting transfers between devices: 9.76 us -> 15 us
    ppermute x2, starting transfers between devices: 0.14 us -> 3.93 us  [local(): recv = lax.ppermute(send, ('grp', 'blk'), pairs)]
    ppermute x2, waiting for transfers between devices: 9.03 us -> 5.27 us  [local(): recv = lax.ppermute(send, ('grp', 'blk'), pairs)]
    ppermute x2, waiting for transfers between devices: 3.81 us -> 0.05 us  [the longest x1 0.05 us: local(): inner = lax.ppermute(slab, 'grp', [(i, i ^ 1) for i in range(groups)])]
    ppermute x2, starting transfers between devices: 3.6 us -> 5.11 us  [the longest x1 4.46 us: local(): inner = lax.ppermute(slab, 'grp', [(i, i ^ 1) for i in range(groups)])]
  transfers between devices with their start and end apart: 9 -> 9, of which waited for: 7 -> 5; matrix products, arithmetic and copies ran while one was open for 0% -> 0% of each run, Pallas kernels for 5% -> 5%
where the time goes in v4:
time: 42.8 us; the launch traced here: 42.6 us
  waiting for transfers between devices  16.2 us (38%)
  starting transfers between devices  15 us (35%)
  Pallas kernels  10.3 us (24%)
  local copies, waits for them, and re-layouts  0.87 us (2%)
    ppermute x3, waiting for transfers between devices, exchange(): lax.ppermute(send, axis, [(i, i ^ masks[i % 2]) for i in range(count)])  10.9 us
    pallas_call x1, Pallas kernels, tensor_parts(): pl.pallas_call(lambda *refs: tensor_kernel(*refs[:8], swap, ny, groups, b...  7.38 us
    ppermute x2, waiting for transfers between devices, local(): recv = lax.ppermute(send, ('grp', 'blk'), pairs)  5.27 us
    ppermute x1, starting transfers between devices, local(): inner = lax.ppermute(slab, 'grp', [(i, i ^ 1) for i in range(groups)])  4.46 us
    ppermute x2, starting transfers between devices, local(): recv = lax.ppermute(send, ('grp', 'blk'), pairs)  3.93 us
    ppermute x1, starting transfers between devices, local(): far = lax.ppermute(slab, 'blk', list(enumerate(turn)))  3.36 us
    ppermute x3, starting transfers between devices, exchange(): lax.ppermute(send, axis, [(i, i ^ masks[i % 2]) for i in range(count)])  2.57 us
    pallas_call x1, Pallas kernels, relay(): pl.pallas_call(lambda *refs: relay_kernel(*refs[:5], norm, blocks, *refs[...  2.04 us
  transfers between devices with their start and end apart: 9, of which 5 were waited for; matrix products, arithmetic and copies ran while one was open for 0% of the time, Pallas kernels for 5%

profile of v4, /device:TPU:0, one launch (start us, length us, event | category | flops | bytes accessed | tf_op | source)
XLA Modules:
  0.0 42.6 jit_solution(1489971838257707105)
XLA Ops:
  0.0 0.8 %slice.31.refs_3_ = bf16[3,64,128]{2,1,0:T(8,128)(2,1)S(1)} slice(bf16[3,2048,128]{2,1,0:T(8,128)(2,1)} %bitcast.5), slice={[0:3], [0:64], [0:128]} | slice | bytes 98304 | tf_op jit(solution)/shard_map/slice | solution.py:276
  0.8 3.4 %collective-permute-start.3 = (bf16[3,64,128]{2,1,0:T(8,128)(2,1)S(1)}, bf16[3,64,128]{2,1,0:T(8,128)(2,1)S(1)}, u32[]{:S(2)}, u32[]{:S(2)}) collective-permute-start(bf16[3,64,128]{2,1,0:T(8,128)(2,1)S(1)} %slice.31.refs_3_), channel_id=1, source_target_pairs={{0,7},{1,2},{2,1},{3,4},{4,3},{5,6},{6,5},{7,0},{8,15},{9,10},{10,... | collective-permute-start | bytes 147464 | tf_op jit(solution)/shard_map/ppermute | solution.py:282
  4.2 0.0 collective-permute-start.2
  4.2 0.7 %collective-permute-start.1 = (bf16[3,64,128]{2,1,0:T(8,128)(2,1)S(1)}, bf16[3,64,128]{2,1,0:T(8,128)(2,1)S(1)}, u32[]{:S(2)}, u32[]{:S(2)}) collective-permute-start(bf16[3,64,128]{2,1,0:T(8,128)(2,1)S(1)} %slice.31.refs_3_), channel_id=1, source_target_pairs={{8,16},{16,8},{9,17},{17,9},{10,18},{18,10},{11,19},{19,11},{12,20... | collective-permute-start | bytes 147464 | tf_op jit(solution)/shard_map/ppermute | solution.py:278
  4.8 4.5 %collective-permute-start = (bf16[3,64,128]{2,1,0:T(8,128)(2,1)S(1)}, bf16[3,64,128]{2,1,0:T(8,128)(2,1)S(1)}, u32[]{:S(2)}, u32[]{:S(2)}) collective-permute-start(bf16[3,64,128]{2,1,0:T(8,128)(2,1)S(1)} %slice.31.refs_3_), channel_id=1, source_target_pairs={{0,8},{8,0},{16,24},{24,16},{1,9},{9,1},{17,25},{25,17},{2,10},{10... | collective-permute-start | bytes 147464 | tf_op jit(solution)/shard_map/ppermute | solution.py:277
  9.3 2.0 %relay.1 = (f32[3,8,256,128]{3,2,1,0:T(8,128)S(1)}, bf16[24,256,128]{2,1,0:T(8,128)(2,1)S(1)}, f32[3,8,128]{2,1,0:T(8,128)S(1)}) custom-call(f32[16]{0:T(128)} %refs_0_.1, bf16[3,2048,128]{2,1,0:T(8,128)(2,1)} %bitcast.6, f32[3,8,128]{2,1,0:T(8,128)} %bitcast.7, s32[8,128]{1,0:T(8,128)} %bitcast.8, s32[8,128]{1,0:T(8,128)} %bitcast.9), custom_call_target="tpu_custom_call" | custom-call | tf_op jit(solution)/shard_map/relay/pallas_call | solution.py:91
  11.3 0.0 collective-permute-done.3.refs_7_
  11.4 0.0 collective-permute-done.2.refs_6_
  11.4 0.0 collective-permute-done.1.refs_5_
  11.4 0.1 collective-permute-done.refs_4_
  11.4 7.4 %tensor_parts.1 = (f32[8,128,256]{2,1,0:T(8,128)S(1)}, bf16[8,128,256]{2,1,0:T(8,128)(2,1)S(1)}) custom-call(f32[3,8,256,128]{3,2,1,0:T(8,128)S(1)} %get-tuple-element.12.refs_0_, bf16[24,256,128]{2,1,0:T(8,128)(2,1)S(1)} %get-tuple-element.13.refs_1_, f32[3,8,128]{2,1,0:T(8,128)S(1)} %get-tuple-element.14.refs_2_, bf16[3,64,128]{2,1,0:T(8,128)(2,1)S(1)} %slice.31.refs_3_, ...), custom_call_target="tpu_custom_call" | custom-call | tf_op jit(solution)/shard_map/tensor_parts/pallas_call | solution.py:206
  18.8 0.1 collective-permute-start.4
  18.9 1.9 %collective-permute-done.4 = bf16[8,128,256]{2,1,0:T(8,128)(2,1)S(1)} collective-permute-done((bf16[8,128,256]{2,1,0:T(8,128)(2,1)S(1)}, bf16[8,128,256]{2,1,0:T(8,128)(2,1)S(1)}, u32[]{:S(2)}, u32[]{:S(2)}) %collective-permute-start.4) | collective-permute-done | bytes 524320 | tf_op jit(solution)/shard_map/ppermute | solution.py:264
  20.8 0.1 convert_add_fusion
  20.9 1.2 %collective-permute-start.5 = (bf16[8,64,256]{2,1,0:T(8,128)(2,1)S(1)}, bf16[8,64,256]{2,1,0:T(8,128)(2,1)S(1)}, u32[]{:S(2)}, u32[]{:S(2)}) collective-permute-start(bf16[8,64,256]{2,1,0:T(8,128)(2,1)S(1)} %slice.43), channel_id=1, source_target_pairs={{0,2},{1,5},{2,0},{3,7},{4,6},{5,1},{6,4},{7,3},{8,10},{9,13},{10,... | collective-permute-start | bytes 786440 | tf_op jit(solution)/shard_map/ppermute | solution.py:264
  22.2 5.2 %collective-permute-done.5 = bf16[8,64,256]{2,1,0:T(8,128)(2,1)S(1)} collective-permute-done((bf16[8,64,256]{2,1,0:T(8,128)(2,1)S(1)}, bf16[8,64,256]{2,1,0:T(8,128)(2,1)S(1)}, u32[]{:S(2)}, u32[]{:S(2)}) %collective-permute-start.5) | collective-permute-done | bytes 262176 | tf_op jit(solution)/shard_map/ppermute | solution.py:264
  27.4 0.1 slice_add_fusion
  27.5 1.3 %collective-permute-start.6 = (bf16[8,32,256]{2,1,0:T(8,128)(2,1)S(1)}, bf16[8,32,256]{2,1,0:T(8,128)(2,1)S(1)}, u32[]{:S(2)}, u32[]{:S(2)}) collective-permute-start(bf16[8,32,256]{2,1,0:T(8,128)(2,1)S(1)} %slice.44), channel_id=1, source_target_pairs={{0,4},{1,3},{2,6},{3,1},{4,0},{5,7},{6,2},{7,5},{8,12},{9,11},{10,... | collective-permute-start | bytes 393224 | tf_op jit(solution)/shard_map/ppermute | solution.py:264
  28.7 3.8 %collective-permute-done.6 = bf16[8,32,256]{2,1,0:T(8,128)(2,1)S(1)} collective-permute-done((bf16[8,32,256]{2,1,0:T(8,128)(2,1)S(1)}, bf16[8,32,256]{2,1,0:T(8,128)(2,1)S(1)}, u32[]{:S(2)}, u32[]{:S(2)}) %collective-permute-start.6) | collective-permute-done | bytes 131104 | tf_op jit(solution)/shard_map/ppermute | solution.py:264
  32.6 2.0 %collective-permute-start.7 = (bf16[8,32,128]{2,1,0:T(8,128)(2,1)S(1)}, bf16[8,32,128]{2,1,0:T(8,128)(2,1)S(1)}, u32[]{:S(2)}, u32[]{:S(2)}) collective-permute-start(bf16[8,32,128]{2,1,0:T(8,128)(2,1)S(1)} %slice.45), channel_id=1, source_target_pairs={{0,8},{1,17},{2,10},{3,19},{4,12},{5,21},{6,14},{7,23},{8,0},{9,25... | collective-permute-start | bytes 196616 | tf_op jit(solution)/shard_map/ppermute | solution.py:329
  34.6 2.3 %collective-permute-done.7.recv_ref = bf16[8,32,128]{2,1,0:T(8,128)(2,1)S(1)} collective-permute-done((bf16[8,32,128]{2,1,0:T(8,128)(2,1)S(1)}, bf16[8,32,128]{2,1,0:T(8,128)(2,1)S(1)}, u32[]{:S(2)}, u32[]{:S(2)}) %collective-permute-start.7) | collective-permute-done | bytes 65568 | tf_op jit(solution)/shard_map/ppermute | solution.py:329
  36.9 0.1 fold.1
  37.0 1.9 %collective-permute-start.8 = (bf16[4,32,128]{2,1,0:T(8,128)(2,1)S(1)}, bf16[4,32,128]{2,1,0:T(8,128)(2,1)S(1)}, u32[]{:S(2)}, u32[]{:S(2)}) collective-permute-start(bf16[4,32,128]{2,1,0:T(8,128)(2,1)S(1)} %get-tuple-element.18), channel_id=1, source_target_pairs={{0,16},{1,9},{2,18},{3,11},{4,20},{5,13},{6,22},{7,15},{8,24},{9,1... | collective-permute-start | bytes 98312 | tf_op jit(solution)/shard_map/ppermute | solution.py:329
  38.9 3.0 %collective-permute-done.8.recv_ref = bf16[4,32,128]{2,1,0:T(8,128)(2,1)S(1)} collective-permute-done((bf16[4,32,128]{2,1,0:T(8,128)(2,1)S(1)}, bf16[4,32,128]{2,1,0:T(8,128)(2,1)S(1)}, u32[]{:S(2)}, u32[]{:S(2)}) %collective-permute-start.8) | collective-permute-done | bytes 32800 | tf_op jit(solution)/shard_map/ppermute | solution.py:329
  41.9 0.7 %finish.1 = f32[8,32,64]{2,1,0:T(8,128)} custom-call(f32[4,32,128]{2,1,0:T(8,128)S(1)} %get-tuple-element.17.keep_ref, bf16[4,32,128]{2,1,0:T(8,128)(2,1)S(1)} %collective-permute-done.8.recv_ref), custom_call_target="tpu_custom_call" | custom-call | tf_op jit(solution)/shard_map/finish/pallas_call | solution.py:254
  (5 shorter events, 0.1 us)
Async XLA Ops:
  0.8 10.5 %collective-permute-start.3 = (bf16[3,64,128]{2,1,0:T(8,128)(2,1)S(1)}, bf16[3,64,128]{2,1,0:T(8,128)(2,1)S(1)}, u32[]{:S(2)}, u32[]{:S(2)}) collective-permute-start(bf16[3,64,128]{2,1,0:T(8,128)(2,1)S(1)} %slice.31.refs_3_), channel_id=1, source_target_pairs={{0,7},{1,2},{2,1},{3,4},{4,3},{5,6},{6,5},{7,0},{8,15},{9,10},{10,... | collective-permute-start | bytes 147464 | tf_op jit(solution)/shard_map/ppermute | solution.py:282
  4.2 7.2 %collective-permute-start.2 = (bf16[3,64,128]{2,1,0:T(8,128)(2,1)S(1)}, bf16[3,64,128]{2,1,0:T(8,128)(2,1)S(1)}, u32[]{:S(2)}, u32[]{:S(2)}) collective-permute-start(bf16[3,64,128]{2,1,0:T(8,128)(2,1)S(1)} %slice.31.refs_3_), channel_id=1, source_target_pairs={{0,1},{1,0},{2,3},{3,2},{4,5},{5,4},{6,7},{7,6},{8,9},{9,8},{10,11... | collective-permute-start | bytes 147464 | tf_op jit(solution)/shard_map/ppermute | solution.py:283
  4.2 7.2 %collective-permute-start.1 = (bf16[3,64,128]{2,1,0:T(8,128)(2,1)S(1)}, bf16[3,64,128]{2,1,0:T(8,128)(2,1)S(1)}, u32[]{:S(2)}, u32[]{:S(2)}) collective-permute-start(bf16[3,64,128]{2,1,0:T(8,128)(2,1)S(1)} %slice.31.refs_3_), channel_id=1, source_target_pairs={{8,16},{16,8},{9,17},{17,9},{10,18},{18,10},{11,19},{19,11},{12,20... | collective-permute-start | bytes 147464 | tf_op jit(solution)/shard_map/ppermute | solution.py:278
  4.8 6.6 %collective-permute-start = (bf16[3,64,128]{2,1,0:T(8,128)(2,1)S(1)}, bf16[3,64,128]{2,1,0:T(8,128)(2,1)S(1)}, u32[]{:S(2)}, u32[]{:S(2)}) collective-permute-start(bf16[3,64,128]{2,1,0:T(8,128)(2,1)S(1)} %slice.31.refs_3_), channel_id=1, source_target_pairs={{0,8},{8,0},{16,24},{24,16},{1,9},{9,1},{17,25},{25,17},{2,10},{10... | collective-permute-start | bytes 147464 | tf_op jit(solution)/shard_map/ppermute | solution.py:277
  18.8 2.0 %collective-permute-start.4 = (bf16[8,128,256]{2,1,0:T(8,128)(2,1)S(1)}, bf16[8,128,256]{2,1,0:T(8,128)(2,1)S(1)}, u32[]{:S(2)}, u32[]{:S(2)}) collective-permute-start(bf16[8,128,256]{2,1,0:T(8,128)(2,1)S(1)} %get-tuple-element.16), channel_id=1, source_target_pairs={{0,1},{1,0},{2,3},{3,2},{4,5},{5,4},{6,7},{7,6},{8,9},{9,8},{10,11... | collective-permute-start | bytes 1572872 | tf_op jit(solution)/shard_map/ppermute | solution.py:264
  20.9 6.4 %collective-permute-start.5 = (bf16[8,64,256]{2,1,0:T(8,128)(2,1)S(1)}, bf16[8,64,256]{2,1,0:T(8,128)(2,1)S(1)}, u32[]{:S(2)}, u32[]{:S(2)}) collective-permute-start(bf16[8,64,256]{2,1,0:T(8,128)(2,1)S(1)} %slice.43), channel_id=1, source_target_pairs={{0,2},{1,5},{2,0},{3,7},{4,6},{5,1},{6,4},{7,3},{8,10},{9,13},{10,... | collective-permute-start | bytes 786440 | tf_op jit(solution)/shard_map/ppermute | solution.py:264
  27.5 5.0 %collective-permute-start.6 = (bf16[8,32,256]{2,1,0:T(8,128)(2,1)S(1)}, bf16[8,32,256]{2,1,0:T(8,128)(2,1)S(1)}, u32[]{:S(2)}, u32[]{:S(2)}) collective-permute-start(bf16[8,32,256]{2,1,0:T(8,128)(2,1)S(1)} %slice.44), channel_id=1, source_target_pairs={{0,4},{1,3},{2,6},{3,1},{4,0},{5,7},{6,2},{7,5},{8,12},{9,11},{10,... | collective-permute-start | bytes 393224 | tf_op jit(solution)/shard_map/ppermute | solution.py:264
  32.6 4.3 %collective-permute-start.7 = (bf16[8,32,128]{2,1,0:T(8,128)(2,1)S(1)}, bf16[8,32,128]{2,1,0:T(8,128)(2,1)S(1)}, u32[]{:S(2)}, u32[]{:S(2)}) collective-permute-start(bf16[8,32,128]{2,1,0:T(8,128)(2,1)S(1)} %slice.45), channel_id=1, source_target_pairs={{0,8},{1,17},{2,10},{3,19},{4,12},{5,21},{6,14},{7,23},{8,0},{9,25... | collective-permute-start | bytes 196616 | tf_op jit(solution)/shard_map/ppermute | solution.py:329
  37.0 4.9 %collective-permute-start.8 = (bf16[4,32,128]{2,1,0:T(8,128)(2,1)S(1)}, bf16[4,32,128]{2,1,0:T(8,128)(2,1)S(1)}, u32[]{:S(2)}, u32[]{:S(2)}) collective-permute-start(bf16[4,32,128]{2,1,0:T(8,128)(2,1)S(1)} %get-tuple-element.18), channel_id=1, source_target_pairs={{0,16},{1,9},{2,18},{3,11},{4,20},{5,13},{6,22},{7,15},{8,24},{9,1... | collective-permute-start | bytes 98312 | tf_op jit(solution)/shard_map/ppermute | solution.py:329

commit v5 on v4

--- a/solution.py
+++ b/solution.py
@@ -13,7 +13,7 @@
 BF16 = jnp.bfloat16
 
 
-def halving_masks(devices, first):
+def halving_bits(devices, first):
     bits = [1 << b for b in range(first, devices.bit_length() - 1)]
     turn = len(bits) // 2
     return [bits, bits[turn:] + bits[:turn]]
@@ -26,23 +26,32 @@
     return table
 
 
+def row_tables(blocks):
+    return [xor_table([bit | 1 for bit in bits]) for bits in halving_bits(blocks, 1)]
+
+
+def column_tables(groups):
+    return [xor_table(bits) for bits in halving_bits(groups, 0)]
+
+
+def regroup(tables):
+    return [tables[0].index(t) for t in tables[1]]
+
+
+def parity(layer, block):
+    value = layer ^ block
+    for shift in (8, 4, 2, 1):
+        value = value ^ (value >> shift)
+    return value & 1
+
+
 def place():
     block, layer = lax.axis_index("blk"), lax.axis_index("grp")
-    return block, layer, block % 2 == 1
-
-
-def adv_order(blocks):
-    block, _, odd = place()
-    near, far = (xor_table(masks) for masks in halving_masks(blocks, 1))
-    even = near + [t ^ 1 for t in far]
-    other = far + [t ^ 1 for t in near]
-    return [block ^ (e if e == o else jnp.where(odd, o, e)) for e, o in zip(even, other)]
-
-
-def test_order(groups):
-    _, layer, odd = place()
-    even, other = (xor_table(masks) for masks in halving_masks(groups, 0))
-    return [layer ^ (e if e == o else jnp.where(odd, o, e)) for e, o in zip(even, other)]
+    return block, layer, parity(layer, block) == 1
+
+
+def ordered(base, tables, flag):
+    return [base ^ (e if e == o else jnp.where(flag, o, e)) for e, o in zip(*tables)]
 
 
 def vmem(shape, dtype):
@@ -62,7 +71,9 @@
     copies = [pltpu.make_async_copy(a, b, sem.at[n]) for n, (a, b) in enumerate(pairs)]
     for copy in copies[4:] + copies[:4]:
         copy.start()
-    order = adv_order(blocks)
+    block, _, flag = place()
+    near = ordered(block, row_tables(blocks), flag)
+    order = near + [n ^ 1 for n in near]
     for c in range(comps):
         copies[4 + c].wait()
         flat_ref[c] = rows_ref[c].astype(F32)
@@ -114,13 +125,14 @@
 
 
 def tensor_kernel(wide_ref, adv_ref, scale_ref, slab_ref, inner_ref, outer_ref, near_ref,
-                  far_ref, swap, ny, groups, blocks, keep_ref, send_ref, grad_ref, t0_ref, t1_ref):
+                  far_ref, swap, row_swap, ny, groups, blocks, keep_ref, send_ref, grad_ref, t0_ref, t1_ref):
     comps, cells, count, _ = wide_ref.shape
     half = keep_ref.shape[1]
     width = count // groups
     tile = min(width, TILE)
-    order = test_order(groups)
-    block, layer, odd = place()
+    block, layer, flag = place()
+    order = ordered(layer, column_tables(groups), flag)
+    odd = block % 2 == 1
     raised = layer % 2 == 1
     row = lax.broadcasted_iota(jnp.int32, (cells, LANES), 0)
     lane = lax.broadcasted_iota(jnp.int32, (cells, LANES), 1)
@@ -179,11 +191,22 @@
         out = lax.dot_general(
             adv, tested, (((1,), (1,)), ((), ())), preferred_element_type=F32
         )
-        keep_ref[k] = out[:half]
-        gone = out[half:]
-        send_ref[k] = jnp.concatenate(
-            [gone[:, s * width : (s + 1) * width] for s in swap], axis=1
-        ).astype(BF16)
+        low, high = out[:half], out[half:]
+        rows = half // len(row_swap)
+        low_far, high_far = (
+            jnp.concatenate([x[n * rows : (n + 1) * rows] for n in row_swap], axis=0)
+            for x in (low, high)
+        )
+
+        def columns(even, other, places):
+            parts = [
+                (other if bin(n).count("1") % 2 else even)[:, n * width : (n + 1) * width]
+                for n in places
+            ]
+            return jnp.concatenate(parts, axis=1)
+
+        keep_ref[k] = columns(low, high, range(groups))
+        send_ref[k] = columns(high_far, low_far, swap).astype(BF16)
 
     build(0, t0_ref)
 
@@ -200,11 +223,11 @@
     contract(KS - 1, t1_ref)
 
 
-def tensor_parts(wide, adv, scale, slabs, swap, ny, groups, blocks):
+def tensor_parts(wide, adv, scale, slabs, swap, row_swap, ny, groups, blocks):
     comps, cells, count, _ = wide.shape
     half = count // 2
     return pl.pallas_call(
-        lambda *refs: tensor_kernel(*refs[:8], swap, ny, groups, blocks, *refs[8:]),
+        lambda *refs: tensor_kernel(*refs[:8], swap, row_swap, ny, groups, blocks, *refs[8:]),
         out_shape=[vmem((KS, half, count), F32), vmem((KS, half, count), BF16)],
         scratch_shapes=[
             pltpu.VMEM((KS * comps * comps, cells, LANES), F32),
@@ -259,9 +282,13 @@
     )(inside(keep), inside(recv))
 
 
-def exchange(send, axis, masks):
-    count = lax.axis_size(axis)
-    return lax.ppermute(send, axis, [(i, i ^ masks[i % 2]) for i in range(count)])
+def exchange(send, groups, blocks, target):
+    pairs = []
+    for g in range(groups):
+        for b in range(blocks):
+            h, c = target(g, b)
+            pairs.append((g * blocks + b, h * blocks + c))
+    return lax.ppermute(send, ("grp", "blk"), pairs)
 
 
 def local(modes, metric, block_map, flags, region_scale):
@@ -274,13 +301,17 @@
 
     rows = modes.reshape(comps, count * cells, nz)
     slab = rows[:, : KS * cells]
-    inner = lax.ppermute(slab, "grp", [(i, i ^ 1) for i in range(groups)])
-    outer = lax.ppermute(
-        slab, "grp", [(i, i + 1 if i % 2 else i - 1) for i in range(1, groups - 1)]
-    )
-    turn = [(i + 1) % blocks if i % 2 else (i - 1) % blocks for i in range(blocks)]
-    far = lax.ppermute(slab, "blk", list(enumerate(turn)))
-    near = lax.ppermute(slab, "blk", [(i, i ^ 1) for i in range(blocks)])
+
+    def outer_of(g, b):
+        return (g + 1 if g % 2 else g - 1, b) if 0 < g < groups - 1 else (g, b ^ 1)
+
+    def far_of(g, b):
+        return g, (b + 1 if b % 2 else b - 1) % blocks
+
+    inner = exchange(slab, groups, blocks, lambda g, b: (g ^ 1, b))
+    outer = exchange(slab, groups, blocks, outer_of)
+    far = exchange(slab, groups, blocks, far_of)
+    near = exchange(slab, groups, blocks, lambda g, b: (g, b ^ 1))
 
     wide, adv, scale = relay(
         region_scale,
@@ -292,28 +323,26 @@
         count,
         blocks,
     )
-    even_masks, odd_masks = halving_masks(groups, 0)
-    even_order = xor_table(even_masks)
-    swap = [even_order.index(t) for t in xor_table(odd_masks)]
     keep, send = tensor_parts(
         wide,
         adv,
         scale,
         (slab, inner, outer, near, far),
-        swap,
+        regroup(column_tables(groups)),
+        regroup(row_tables(blocks)),
         ny,
         groups,
         blocks,
     )
 
-    recv = exchange(send, "blk", [1, 1])
-    for masks in zip(*halving_masks(blocks, 1)):
+    recv = exchange(send, groups, blocks, lambda g, b: (g, b ^ 1))
+    for bits in zip(*halving_bits(blocks, 1)):
         total = keep + recv.astype(F32)
         half = total.shape[1] // 2
         keep, send = total[:, :half], total[:, half:].astype(BF16)
-        recv = exchange(send, "blk", masks)
+        recv = exchange(send, groups, blocks, lambda g, b: (g, b ^ bits[parity(g, b)] ^ 1))
     width = count
-    for masks in zip(even_masks, odd_masks):
+    for bits in zip(*halving_bits(groups, 0)):
         if width > LANES:
             total = keep + recv.astype(F32)
             half = width // 2
@@ -321,12 +350,7 @@
         else:
             keep, send = fold(keep, recv, width)
         width //= 2
-        pairs = [
-            (g * blocks + b, (g ^ masks[b % 2]) * blocks + b)
-            for g in range(groups)
-            for b in range(blocks)
-        ]
-        recv = lax.ppermute(send, ("grp", "blk"), pairs)
+        recv = exchange(send, groups, blocks, lambda g, b: (g ^ bits[parity(g, b)], b ^ 1))
     return jnp.swapaxes(finish(keep, recv, width), 1, 2)
 
 

time: 42.8 us -> 38.5 us (0.90)
  starting transfers between devices: 15 us -> 12.2 us
  waiting for transfers between devices: 16.2 us -> 14.7 us
    ppermute x9, starting transfers between devices: 15 us -> 12.2 us  [exchange(): return lax.ppermute(send, ('grp', 'blk'), pairs)]
    ppermute x9, waiting for transfers between devices: 16.2 us -> 14.7 us  [exchange(): return lax.ppermute(send, ('grp', 'blk'), pairs)]
where the time goes in v5:
time: 38.5 us; the launch traced here: 38.3 us
  waiting for transfers between devices  14.7 us (38%)
  starting transfers between devices  12.2 us (32%)
  Pallas kernels  10.1 us (26%)
  local copies, waits for them, and re-layouts  0.87 us (2%)
    ppermute x9, waiting for transfers between devices, exchange(): return lax.ppermute(send, ('grp', 'blk'), pairs)  14.7 us
    ppermute x9, starting transfers between devices, exchange(): return lax.ppermute(send, ('grp', 'blk'), pairs)  12.2 us
    pallas_call x1, Pallas kernels, tensor_parts(): pl.pallas_call(lambda *refs: tensor_kernel(*refs[:8], swap, row_swap, ny,...  7.25 us
    pallas_call x1, Pallas kernels, relay(): pl.pallas_call(lambda *refs: relay_kernel(*refs[:5], norm, blocks, *refs[...  2.04 us
    slice x1, local copies, waits for them, and re-layouts, local(): slab = rows[:, :KS * cells]  0.8 us
  transfers between devices with their start and end apart: 9, of which 5 were waited for; matrix products, arithmetic and copies ran while one was open for 0% of the time, Pallas kernels for 5%

profile of v5, /device:TPU:0, one launch (start us, length us, event | category | flops | bytes accessed | tf_op | source)
XLA Modules:
  0.0 38.3 jit_solution(12879912817806760695)
XLA Ops:
  0.0 0.8 %slice.31.refs_3_ = bf16[3,64,128]{2,1,0:T(8,128)(2,1)S(1)} slice(bf16[3,2048,128]{2,1,0:T(8,128)(2,1)} %bitcast.5), slice={[0:3], [0:64], [0:128]} | slice | bytes 98304 | tf_op jit(solution)/shard_map/slice | solution.py:303
  0.8 3.4 %collective-permute-start.3 = (bf16[3,64,128]{2,1,0:T(8,128)(2,1)S(1)}, bf16[3,64,128]{2,1,0:T(8,128)(2,1)S(1)}, u32[]{:S(2)}, u32[]{:S(2)}) collective-permute-start(bf16[3,64,128]{2,1,0:T(8,128)(2,1)S(1)} %slice.31.refs_3_), channel_id=1, source_target_pairs={{0,7},{1,2},{2,1},{3,4},{4,3},{5,6},{6,5},{7,0},{8,15},{9,10},{10,... | collective-permute-start | bytes 147464 | tf_op jit(solution)/shard_map/ppermute | solution.py:291
  4.2 0.0 collective-permute-start.2
  4.2 0.5 %collective-permute-start.1 = (bf16[3,64,128]{2,1,0:T(8,128)(2,1)S(1)}, bf16[3,64,128]{2,1,0:T(8,128)(2,1)S(1)}, u32[]{:S(2)}, u32[]{:S(2)}) collective-permute-start(bf16[3,64,128]{2,1,0:T(8,128)(2,1)S(1)} %slice.31.refs_3_), channel_id=1, source_target_pairs={{0,1},{1,0},{2,3},{3,2},{4,5},{5,4},{6,7},{7,6},{8,16},{9,17},{10,... | collective-permute-start | bytes 147464 | tf_op jit(solution)/shard_map/ppermute | solution.py:291
  4.7 2.6 %collective-permute-start = (bf16[3,64,128]{2,1,0:T(8,128)(2,1)S(1)}, bf16[3,64,128]{2,1,0:T(8,128)(2,1)S(1)}, u32[]{:S(2)}, u32[]{:S(2)}) collective-permute-start(bf16[3,64,128]{2,1,0:T(8,128)(2,1)S(1)} %slice.31.refs_3_), channel_id=1, source_target_pairs={{0,8},{1,9},{2,10},{3,11},{4,12},{5,13},{6,14},{7,15},{8,0},{9,1},... | collective-permute-start | bytes 147464 | tf_op jit(solution)/shard_map/ppermute | solution.py:291
  7.3 2.0 %relay.1 = (f32[3,8,256,128]{3,2,1,0:T(8,128)S(1)}, bf16[24,256,128]{2,1,0:T(8,128)(2,1)S(1)}, f32[3,8,128]{2,1,0:T(8,128)S(1)}) custom-call(f32[16]{0:T(128)} %refs_0_.1, bf16[3,2048,128]{2,1,0:T(8,128)(2,1)} %bitcast.6, f32[3,8,128]{2,1,0:T(8,128)} %bitcast.7, s32[8,128]{1,0:T(8,128)} %bitcast.8, s32[8,128]{1,0:T(8,128)} %bitcast.9), custom_call_target="tpu_custom_call" | custom-call | tf_op jit(solution)/shard_map/relay/pallas_call | solution.py:102
  9.4 0.0 collective-permute-done.3.refs_7_
  9.4 0.0 collective-permute-done.2.refs_6_
  9.4 0.0 collective-permute-done.1.refs_5_
  9.4 0.0 collective-permute-done.refs_4_
  9.5 7.2 %tensor_parts.1 = (f32[8,128,256]{2,1,0:T(8,128)S(1)}, bf16[8,128,256]{2,1,0:T(8,128)(2,1)S(1)}) custom-call(f32[3,8,256,128]{3,2,1,0:T(8,128)S(1)} %get-tuple-element.12.refs_0_, bf16[24,256,128]{2,1,0:T(8,128)(2,1)S(1)} %get-tuple-element.13.refs_1_, f32[3,8,128]{2,1,0:T(8,128)S(1)} %get-tuple-element.14.refs_2_, bf16[3,64,128]{2,1,0:T(8,128)(2,1)S(1)} %slice.31.refs_3_, ...), custom_call_target="tpu_custom_call" | custom-call | tf_op jit(solution)/shard_map/tensor_parts/pallas_call | solution.py:229
  16.7 0.1 collective-permute-start.4
  16.8 1.9 %collective-permute-done.4 = bf16[8,128,256]{2,1,0:T(8,128)(2,1)S(1)} collective-permute-done((bf16[8,128,256]{2,1,0:T(8,128)(2,1)S(1)}, bf16[8,128,256]{2,1,0:T(8,128)(2,1)S(1)}, u32[]{:S(2)}, u32[]{:S(2)}) %collective-permute-start.4) | collective-permute-done | bytes 524320 | tf_op jit(solution)/shard_map/ppermute | solution.py:291
  18.7 0.1 convert_add_fusion
  18.8 1.0 %collective-permute-start.5 = (bf16[8,64,256]{2,1,0:T(8,128)(2,1)S(1)}, bf16[8,64,256]{2,1,0:T(8,128)(2,1)S(1)}, u32[]{:S(2)}, u32[]{:S(2)}) collective-permute-start(bf16[8,64,256]{2,1,0:T(8,128)(2,1)S(1)} %slice.43), channel_id=1, source_target_pairs={{0,3},{1,4},{2,7},{3,0},{4,1},{5,6},{6,5},{7,2},{8,13},{9,10},{10,... | collective-permute-start | bytes 786440 | tf_op jit(solution)/shard_map/ppermute | solution.py:291
  19.8 4.9 %collective-permute-done.5 = bf16[8,64,256]{2,1,0:T(8,128)(2,1)S(1)} collective-permute-done((bf16[8,64,256]{2,1,0:T(8,128)(2,1)S(1)}, bf16[8,64,256]{2,1,0:T(8,128)(2,1)S(1)}, u32[]{:S(2)}, u32[]{:S(2)}) %collective-permute-start.5) | collective-permute-done | bytes 262176 | tf_op jit(solution)/shard_map/ppermute | solution.py:291
  24.7 0.1 slice_add_fusion
  24.8 1.0 %collective-permute-start.6 = (bf16[8,32,256]{2,1,0:T(8,128)(2,1)S(1)}, bf16[8,32,256]{2,1,0:T(8,128)(2,1)S(1)}, u32[]{:S(2)}, u32[]{:S(2)}) collective-permute-start(bf16[8,32,256]{2,1,0:T(8,128)(2,1)S(1)} %slice.44), channel_id=1, source_target_pairs={{0,5},{1,2},{2,1},{3,6},{4,7},{5,0},{6,3},{7,4},{8,11},{9,12},{10,... | collective-permute-start | bytes 393224 | tf_op jit(solution)/shard_map/ppermute | solution.py:291
  25.8 3.4 %collective-permute-done.6 = bf16[8,32,256]{2,1,0:T(8,128)(2,1)S(1)} collective-permute-done((bf16[8,32,256]{2,1,0:T(8,128)(2,1)S(1)}, bf16[8,32,256]{2,1,0:T(8,128)(2,1)S(1)}, u32[]{:S(2)}, u32[]{:S(2)}) %collective-permute-start.6) | collective-permute-done | bytes 131104 | tf_op jit(solution)/shard_map/ppermute | solution.py:291
  29.3 1.8 %collective-permute-start.7 = (bf16[8,32,128]{2,1,0:T(8,128)(2,1)S(1)}, bf16[8,32,128]{2,1,0:T(8,128)(2,1)S(1)}, u32[]{:S(2)}, u32[]{:S(2)}) collective-permute-start(bf16[8,32,128]{2,1,0:T(8,128)(2,1)S(1)} %slice.45), channel_id=1, source_target_pairs={{0,9},{1,16},{2,19},{3,10},{4,21},{5,12},{6,15},{7,22},{8,25},{9,0... | collective-permute-start | bytes 196616 | tf_op jit(solution)/shard_map/ppermute | solution.py:291
  31.1 2.0 %collective-permute-done.7.recv_ref = bf16[8,32,128]{2,1,0:T(8,128)(2,1)S(1)} collective-permute-done((bf16[8,32,128]{2,1,0:T(8,128)(2,1)S(1)}, bf16[8,32,128]{2,1,0:T(8,128)(2,1)S(1)}, u32[]{:S(2)}, u32[]{:S(2)}) %collective-permute-start.7) | collective-permute-done | bytes 65568 | tf_op jit(solution)/shard_map/ppermute | solution.py:291
  33.1 0.1 fold.1
  33.2 1.9 %collective-permute-start.8 = (bf16[4,32,128]{2,1,0:T(8,128)(2,1)S(1)}, bf16[4,32,128]{2,1,0:T(8,128)(2,1)S(1)}, u32[]{:S(2)}, u32[]{:S(2)}) collective-permute-start(bf16[4,32,128]{2,1,0:T(8,128)(2,1)S(1)} %get-tuple-element.18), channel_id=1, source_target_pairs={{0,17},{1,8},{2,11},{3,18},{4,13},{5,20},{6,23},{7,14},{8,1},{9,24... | collective-permute-start | bytes 98312 | tf_op jit(solution)/shard_map/ppermute | solution.py:291
  35.1 2.4 %collective-permute-done.8.recv_ref = bf16[4,32,128]{2,1,0:T(8,128)(2,1)S(1)} collective-permute-done((bf16[4,32,128]{2,1,0:T(8,128)(2,1)S(1)}, bf16[4,32,128]{2,1,0:T(8,128)(2,1)S(1)}, u32[]{:S(2)}, u32[]{:S(2)}) %collective-permute-start.8) | collective-permute-done | bytes 32800 | tf_op jit(solution)/shard_map/ppermute | solution.py:291
  37.5 0.7 %finish.1 = f32[8,32,64]{2,1,0:T(8,128)} custom-call(f32[4,32,128]{2,1,0:T(8,128)S(1)} %get-tuple-element.17.keep_ref, bf16[4,32,128]{2,1,0:T(8,128)(2,1)S(1)} %collective-permute-done.8.recv_ref), custom_call_target="tpu_custom_call" | custom-call | tf_op jit(solution)/shard_map/finish/pallas_call | solution.py:277
  (5 shorter events, 0.1 us)
Async XLA Ops:
  0.8 8.6 %collective-permute-start.3 = (bf16[3,64,128]{2,1,0:T(8,128)(2,1)S(1)}, bf16[3,64,128]{2,1,0:T(8,128)(2,1)S(1)}, u32[]{:S(2)}, u32[]{:S(2)}) collective-permute-start(bf16[3,64,128]{2,1,0:T(8,128)(2,1)S(1)} %slice.31.refs_3_), channel_id=1, source_target_pairs={{0,7},{1,2},{2,1},{3,4},{4,3},{5,6},{6,5},{7,0},{8,15},{9,10},{10,... | collective-permute-start | bytes 147464 | tf_op jit(solution)/shard_map/ppermute | solution.py:291
  4.2 5.2 %collective-permute-start.2 = (bf16[3,64,128]{2,1,0:T(8,128)(2,1)S(1)}, bf16[3,64,128]{2,1,0:T(8,128)(2,1)S(1)}, u32[]{:S(2)}, u32[]{:S(2)}) collective-permute-start(bf16[3,64,128]{2,1,0:T(8,128)(2,1)S(1)} %slice.31.refs_3_), channel_id=1, source_target_pairs={{0,1},{1,0},{2,3},{3,2},{4,5},{5,4},{6,7},{7,6},{8,9},{9,8},{10,11... | collective-permute-start | bytes 147464 | tf_op jit(solution)/shard_map/ppermute | solution.py:291
  4.2 5.2 %collective-permute-start.1 = (bf16[3,64,128]{2,1,0:T(8,128)(2,1)S(1)}, bf16[3,64,128]{2,1,0:T(8,128)(2,1)S(1)}, u32[]{:S(2)}, u32[]{:S(2)}) collective-permute-start(bf16[3,64,128]{2,1,0:T(8,128)(2,1)S(1)} %slice.31.refs_3_), channel_id=1, source_target_pairs={{0,1},{1,0},{2,3},{3,2},{4,5},{5,4},{6,7},{7,6},{8,16},{9,17},{10,... | collective-permute-start | bytes 147464 | tf_op jit(solution)/shard_map/ppermute | solution.py:291
  4.7 4.8 %collective-permute-start = (bf16[3,64,128]{2,1,0:T(8,128)(2,1)S(1)}, bf16[3,64,128]{2,1,0:T(8,128)(2,1)S(1)}, u32[]{:S(2)}, u32[]{:S(2)}) collective-permute-start(bf16[3,64,128]{2,1,0:T(8,128)(2,1)S(1)} %slice.31.refs_3_), channel_id=1, source_target_pairs={{0,8},{1,9},{2,10},{3,11},{4,12},{5,13},{6,14},{7,15},{8,0},{9,1},... | collective-permute-start | bytes 147464 | tf_op jit(solution)/shard_map/ppermute | solution.py:291
  16.7 2.0 %collective-permute-start.4 = (bf16[8,128,256]{2,1,0:T(8,128)(2,1)S(1)}, bf16[8,128,256]{2,1,0:T(8,128)(2,1)S(1)}, u32[]{:S(2)}, u32[]{:S(2)}) collective-permute-start(bf16[8,128,256]{2,1,0:T(8,128)(2,1)S(1)} %get-tuple-element.16), channel_id=1, source_target_pairs={{0,1},{1,0},{2,3},{3,2},{4,5},{5,4},{6,7},{7,6},{8,9},{9,8},{10,11... | collective-permute-start | bytes 1572872 | tf_op jit(solution)/shard_map/ppermute | solution.py:291
  18.8 5.9 %collective-permute-start.5 = (bf16[8,64,256]{2,1,0:T(8,128)(2,1)S(1)}, bf16[8,64,256]{2,1,0:T(8,128)(2,1)S(1)}, u32[]{:S(2)}, u32[]{:S(2)}) collective-permute-start(bf16[8,64,256]{2,1,0:T(8,128)(2,1)S(1)} %slice.43), channel_id=1, source_target_pairs={{0,3},{1,4},{2,7},{3,0},{4,1},{5,6},{6,5},{7,2},{8,13},{9,10},{10,... | collective-permute-start | bytes 786440 | tf_op jit(solution)/shard_map/ppermute | solution.py:291
  24.8 4.5 %collective-permute-start.6 = (bf16[8,32,256]{2,1,0:T(8,128)(2,1)S(1)}, bf16[8,32,256]{2,1,0:T(8,128)(2,1)S(1)}, u32[]{:S(2)}, u32[]{:S(2)}) collective-permute-start(bf16[8,32,256]{2,1,0:T(8,128)(2,1)S(1)} %slice.44), channel_id=1, source_target_pairs={{0,5},{1,2},{2,1},{3,6},{4,7},{5,0},{6,3},{7,4},{8,11},{9,12},{10,... | collective-permute-start | bytes 393224 | tf_op jit(solution)/shard_map/ppermute | solution.py:291
  29.3 3.8 %collective-permute-start.7 = (bf16[8,32,128]{2,1,0:T(8,128)(2,1)S(1)}, bf16[8,32,128]{2,1,0:T(8,128)(2,1)S(1)}, u32[]{:S(2)}, u32[]{:S(2)}) collective-permute-start(bf16[8,32,128]{2,1,0:T(8,128)(2,1)S(1)} %slice.45), channel_id=1, source_target_pairs={{0,9},{1,16},{2,19},{3,10},{4,21},{5,12},{6,15},{7,22},{8,25},{9,0... | collective-permute-start | bytes 196616 | tf_op jit(solution)/shard_map/ppermute | solution.py:291
  33.2 4.3 %collective-permute-start.8 = (bf16[4,32,128]{2,1,0:T(8,128)(2,1)S(1)}, bf16[4,32,128]{2,1,0:T(8,128)(2,1)S(1)}, u32[]{:S(2)}, u32[]{:S(2)}) collective-permute-start(bf16[4,32,128]{2,1,0:T(8,128)(2,1)S(1)} %get-tuple-element.18), channel_id=1, source_target_pairs={{0,17},{1,8},{2,11},{3,18},{4,13},{5,20},{6,23},{7,14},{8,1},{9,24... | collective-permute-start | bytes 98312 | tf_op jit(solution)/shard_map/ppermute | solution.py:291
